TPU v7x, 256 devices: a whole 4x4x8 slice. The times are simulated.
256 devices in a mesh: exp: 32 (over z_hi, y, core), et: 8 (over z_lo, x).
Axes of the slice: x: 4, y: 4, z: 8 (z_hi: 4, z_lo: 2; z = z_hi * 2 + z_lo), core: 2. Of those that a mesh axis runs over, the one named last changes fastest.
Arguments:
- tokens: bfloat16 [1536, 7168], P(('exp', 'et')), may hold values from -6 to 6
- grad_out: bfloat16 [1536, 7168], P(('exp', 'et')), may hold values from -6 to 6
- gates: bfloat16 [1536, 8], P(('exp', 'et')), may hold values from 0.049804688 to 1
- expert_ids: int32 [1536, 8], P(('exp', 'et')), may hold values from 0 to 31, all different within a row; in each aligned block of 6 rows (0 to 5, 6 to 11, ...) at most 2 rows name the same one
- gate_weight: bfloat16 [32, 7168, 1024], P('exp', None, 'et'), may hold values from -0.0625 to 0.0625
- up_weight: bfloat16 [32, 7168, 1024], P('exp', None, 'et'), may hold values from -0.0625 to 0.0625
- down_weight: bfloat16 [32, 1024, 7168], P('exp', 'et'), may hold values from -0.1875 to 0.1875
Outputs:
- input_grad: bfloat16 [1536, 7168], P(('exp', 'et'))
- gate_grad: float32 [1536, 8], P(('exp', 'et'))
- gate_weight_grad: bfloat16 [32, 7168, 1024], P('exp', None, 'et')
- up_weight_grad: bfloat16 [32, 7168, 1024], P('exp', None, 'et')
- down_weight_grad: bfloat16 [32, 1024, 7168], P('exp', 'et')
Inputs may be any that keep to these rules, and one draw needn't show every extreme that they name: `expert_ids`: each row names 8 different experts. Among the 6 tokens of one device no expert is named by more than 2 tokens, and in every draw some expert is named by exactly 2 tokens of some device.
All inputs are finite; a program needn't handle non-finite values.
Results may differ from a plain program's by a relative error of at most 0.017.
Values may be sent and summed in bfloat16 or wider, within the bound.
A program may use at most 128 MiB of HBM per device.

v0:
```python
import jax
import jax.numpy as jnp
from jax import lax
from jax.sharding import PartitionSpec as P

TOP = 8
EXP_DEV = 1


def expert_terms(rows_x, rows_dy, rows_g, w_gate, w_up, w_down):
    gate_pre = jnp.dot(rows_x, w_gate, preferred_element_type=jnp.float32)
    up_pre = jnp.dot(rows_x, w_up, preferred_element_type=jnp.float32)
    sigma = jax.nn.sigmoid(gate_pre)
    silu_val = gate_pre * sigma
    act = silu_val * up_pre
    back = lax.dot_general(
        rows_dy, w_down, (((1,), (1,)), ((), ())), preferred_element_type=jnp.float32
    )
    score = jnp.sum(act * back, axis=1)
    scale = rows_g.astype(jnp.float32)[:, None]
    weighted = (scale * act).astype(jnp.bfloat16)
    dact = scale * back
    grad_gate = (dact * up_pre * sigma * (1.0 + gate_pre * (1.0 - sigma))).astype(jnp.bfloat16)
    grad_up = (dact * silu_val).astype(jnp.bfloat16)
    inward = lax.dot_general(
        grad_gate, w_gate, (((1,), (1,)), ((), ())), preferred_element_type=jnp.float32
    )
    inward = inward + lax.dot_general(
        grad_up, w_up, (((1,), (1,)), ((), ())), preferred_element_type=jnp.float32
    )
    d_gate = lax.dot_general(
        rows_x, grad_gate, (((0,), (0,)), ((), ())), preferred_element_type=jnp.float32
    )
    d_up = lax.dot_general(
        rows_x, grad_up, (((0,), (0,)), ((), ())), preferred_element_type=jnp.float32
    )
    d_down = lax.dot_general(
        weighted, rows_dy, (((0,), (0,)), ((), ())), preferred_element_type=jnp.float32
    )
    return (d_gate, d_up, d_down, inward, score)


def slot_table(routes, experts, width):
    flat = routes.reshape(-1)
    onehot = (flat[:, None] == jnp.arange(experts, dtype=jnp.int32)[None, :]).astype(jnp.int32)
    before = jnp.cumsum(onehot, axis=0) - onehot
    rank = jnp.sum(before * onehot, axis=1)
    return flat * width + rank


def pack_rows(values, slots, total):
    return jnp.zeros((total,) + values.shape[1:], values.dtype).at[slots].set(values)


def build_buffers(owned_x, owned_dy, owned_g, slots, total, n_exp, block):
    depth = owned_x.shape[1]
    buf_x = pack_rows(jnp.repeat(owned_x, TOP, axis=0), slots, total).reshape(n_exp, block, depth)
    buf_dy = pack_rows(jnp.repeat(owned_dy, TOP, axis=0), slots, total).reshape(n_exp, block, depth)
    buf_g = pack_rows(owned_g.reshape(-1), slots, total).reshape(n_exp, block)
    return (buf_x, buf_dy, buf_g)


def on_device(tokens, grad_out, gates, expert_ids, gate_weight, up_weight, down_weight):
    count = tokens.shape[0]
    depth = tokens.shape[1]
    ff_dev = gate_weight.shape[2]
    n_exp = lax.axis_size("exp")
    n_et = lax.axis_size("et")
    experts = n_exp * EXP_DEV
    capacity = max(2, (count * TOP + experts - 1) // experts)
    total = experts * capacity
    slots = slot_table(expert_ids, experts, capacity)
    buf_x, buf_dy, buf_g = build_buffers(
        tokens, grad_out, gates, slots, total, n_exp, EXP_DEV * capacity
    )
    got_x, got_dy, got_g = (
        lax.all_to_all(buf_x, "exp", split_axis=0, concat_axis=0, tiled=True),
        lax.all_to_all(buf_dy, "exp", split_axis=0, concat_axis=0, tiled=True),
        lax.all_to_all(buf_g, "exp", split_axis=0, concat_axis=0, tiled=True),
    )
    got_x = got_x.reshape(n_exp, EXP_DEV, capacity, depth)
    got_dy = got_dy.reshape(n_exp, EXP_DEV, capacity, depth)
    got_g = got_g.reshape(n_exp, EXP_DEV, capacity)
    rows_x = got_x[:, 0].reshape(n_exp * capacity, depth)
    rows_dy = got_dy[:, 0].reshape(n_exp * capacity, depth)
    rows_g = got_g[:, 0].reshape(n_exp * capacity)
    w_gate = gate_weight[0]
    w_up = up_weight[0]
    w_down = down_weight[0]
    height = rows_x.shape[0]

    def accumulate(carry, piece, start, w_gate=w_gate, w_up=w_up, w_down=w_down):
        terms = expert_terms(piece[0], piece[1], piece[2], w_gate, w_up, w_down)
        inward = terms[3]
        score = terms[4]
        return (terms[0], terms[1], terms[2], inward, score)

    init = (
        jnp.zeros((depth, ff_dev), jnp.float32),
        jnp.zeros((depth, ff_dev), jnp.float32),
        jnp.zeros((ff_dev, depth), jnp.float32),
        jnp.zeros((n_et * height, depth), jnp.float32),
        jnp.zeros((n_et * height,), jnp.float32),
    )
    folded = accumulate(
        init,
        (
            lax.all_gather(rows_x, "et", axis=0, tiled=True),
            lax.all_gather(rows_dy, "et", axis=0, tiled=True),
            lax.all_gather(rows_g, "et", axis=0, tiled=True),
        ),
        jnp.int32(0),
    )
    own_part = lax.psum_scatter(
        folded[3].astype(jnp.bfloat16), "et", scatter_dimension=0, tiled=True
    ).astype(jnp.float32)
    own_score = lax.psum_scatter(
        folded[4].astype(jnp.bfloat16), "et", scatter_dimension=0, tiled=True
    ).astype(jnp.float32)
    grads_gate = [folded[0].astype(jnp.bfloat16)]
    grads_up = [folded[1].astype(jnp.bfloat16)]
    grads_down = [folded[2].astype(jnp.bfloat16)]
    parts = [own_part.reshape(n_exp, capacity, depth)]
    scores = [own_score.reshape(n_exp, capacity)]
    part_all = jnp.stack(parts, axis=1).reshape(n_exp, EXP_DEV * capacity, depth)
    score_all = jnp.stack(scores, axis=1).reshape(n_exp, EXP_DEV * capacity)
    back_part, back_score = (
        lax.all_to_all(
            part_all.astype(jnp.bfloat16), "exp", split_axis=0, concat_axis=0, tiled=True
        ).astype(part_all.dtype),
        lax.all_to_all(
            score_all.astype(jnp.bfloat16), "exp", split_axis=0, concat_axis=0, tiled=True
        ).astype(score_all.dtype),
    )
    pair_grad = back_part.reshape(total, depth)[slots].reshape(count, TOP, depth)
    input_grad = jnp.sum(pair_grad, axis=1).astype(jnp.bfloat16)
    gate_grad = back_score.reshape(total)[slots].reshape(count, TOP)
    return (
        input_grad,
        gate_grad,
        jnp.stack(grads_gate, axis=0),
        jnp.stack(grads_up, axis=0),
        jnp.stack(grads_down, axis=0),
    )


def solution(mesh):
    placed = (
        P(("exp", "et"), None),
        P(("exp", "et"), None),
        P(("exp", "et"), None),
        P(("exp", "et"), None),
        P("exp", None, "et"),
        P("exp", None, "et"),
        P("exp", "et", None),
    )
    return jax.shard_map(
        on_device,
        mesh=mesh,
        in_specs=placed,
        out_specs=(
            P(("exp", "et"), None),
            P(("exp", "et"), None),
            P("exp", None, "et"),
            P("exp", None, "et"),
            P("exp", "et", None),
        ),
        check_vma=False,
    )
```

profile of v0, /device:TPU:32, one launch (start us, length us, event | category | flops | bytes accessed | tf_op | source)
XLA Modules:
  0.0 418.0 jit_solution(7645108906760977807)
XLA Ops:
  9.2 2.9 scatter_custom_fusion.2
  14.5 35.4 %all_to_all.31 = bf16[32,2,7168]{2,1,0:T(2,128)(2,1)} all-to-all(bf16[32,2,7168]{2,1,0:T(2,128)(2,1)S(1)} %reshape.95), channel_id=1, replica_groups=mesh['exp'=32,'et'=8] {'exp'}, dimensions={0} | all-to-all | bytes 1835008 | tf_op jit(solution)/shard_map/all_to_all | solution.py:77
  49.9 3.2 reshape_squeeze_reshape.11
  58.0 42.3 %all_to_all.32 = bf16[32,2,7168]{2,1,0:T(2,128)(2,1)} all-to-all(bf16[32,2,7168]{2,1,0:T(2,128)(2,1)S(1)} %reshape.93), channel_id=1, replica_groups=mesh['exp'=32,'et'=8] {'exp'}, dimensions={0} | all-to-all | bytes 1835008 | tf_op jit(solution)/shard_map/all_to_all | solution.py:78
  100.4 3.2 reshape_squeeze_reshape.10
  105.3 4.7 %all-to-all-start = ((bf16[32,1,2]{2,1,0:T(2,128)(2,1)}), bf16[32,1,2]{2,1,0:T(2,128)(2,1)S(1)}, u32[]{:S(2)}, u32[]{:S(2)}) async-start(bf16[32,1,2]{2,1,0:T(2,128)(2,1)} %all_to_all.25), calls=%async_computation | async-start | bytes 32768 | tf_op jit(solution)/shard_map/all_to_all | solution.py:79
  111.5 8.4 %all-to-all-done = bf16[32,1,2]{2,1,0:T(2,128)(2,1)S(1)} async-done(((bf16[32,1,2]{2,1,0:T(2,128)(2,1)}), bf16[32,1,2]{2,1,0:T(2,128)(2,1)S(1)}, u32[]{:S(2)}, u32[]{:S(2)}) %all-to-all-start) | async-done | bytes 160 | tf_op jit(solution)/shard_map/all_to_all | solution.py:79
  120.3 34.9 %all-gather.5.cloned.1.call-done = bf16[512,7168]{1,0:T(8,128)(2,1)} async-done(((bf16[64,7168]{1,0:T(8,128)(2,1)}), bf16[512,7168]{1,0:T(8,128)(2,1)}) %all-gather.5.cloned.1.call-update) | async-done | bytes 7340048 | tf_op jit(solution)/shard_map/all_gather | solution.py:108
  155.2 5.8 %fusion.5 = f32[512,128]{0,1:T(8,128)S(1)} fusion(bf16[512,7168]{1,0:T(8,128)(2,1)} %all-gather.5.cloned.1.call-done, bf16[1,7168,128]{2,1,0:T(8,128)(2,1)S(1)} %copy-done), kind=kOutput, calls=%fused_computation.14 | convolution fusion | flops 939524096 | bytes 9437184 | tf_op jit(solution)/shard_map/dot_general | solution.py:11
  161.0 2.5 fusion.8
  163.5 76.6 %all-gather.3.cloned.1.call-done = bf16[512,7168]{1,0:T(8,128)(2,1)} async-done(((bf16[64,7168]{1,0:T(8,128)(2,1)}), bf16[512,7168]{1,0:T(8,128)(2,1)}) %all-gather.3.cloned.1.call-update) | async-done | bytes 7340048 | tf_op jit(solution)/shard_map/all_gather | solution.py:109
  240.2 6.2 %multiply_reduce_fusion = (bf16[512]{0:T(512)(128)(2,1)S(1)}, f32[512,128]{0,1:T(8,128)S(1)}) fusion(f32[512,128]{0,1:T(8,128)S(1)} %fusion.8, f32[512,128]{0,1:T(8,128)S(1)} %fusion.5, bf16[512,7168]{1,0:T(8,128)(2,1)} %all-gather.3.cloned.1.call-done, bf16[1,128,7168]{2,1,0:T(8,128)(2,1)} %param.13), kind=kOutput, calls=%fused_computation.31 | convolution fusion | flops 939982336 | bytes 9962496 | tf_op jit(solution)/shard_map/dot_general | solution.py:16
  246.4 17.5 %all-reduce.2 = (bf16[512]{0:T(512)(128)(2,1)S(1)}, bf16[512]{0:T(512)(128)(2,1)S(1)}) all-reduce(bf16[512]{0:T(512)(128)(2,1)S(1)} %dynamic-update-slice, bf16[512]{0:T(512)(128)(2,1)S(1)} %get-tuple-element.11), channel_id=1, replica_groups=mesh['exp'=32,'et'=8] {'et'}, use_global_device_ids=true, to_apply=%add | all-reduce | flops 1024 | bytes 4096
  264.0 7.3 %fusion.3 = f32[512,7168]{1,0:T(8,128)} fusion(bf16[512,128]{0,1:T(8,128)(2,1)S(1)} %get-tuple-element.8, bf16[1,7168,128]{2,1,0:T(8,128)(2,1)S(1)} %copy-done), kind=kOutput, calls=%fused_computation.12 | convolution fusion | flops 939524096 | bytes 16646144 | tf_op jit(solution)/shard_map/dot_general | solution.py:25
  271.4 10.3 %add_convert_fusion = bf16[512,7168]{1,0:T(8,128)(2,1)} fusion(f32[512,7168]{1,0:T(8,128)} %fusion.3, bf16[512,128]{0,1:T(8,128)(2,1)S(1)} %get-tuple-element.7, bf16[1,7168,128]{2,1,0:T(8,128)(2,1)S(1)} %copy-done.3), kind=kOutput, calls=%fused_computation.5 | convolution fusion | flops 946864128 | bytes 23986176 | tf_op jit(solution)/shard_map/dot_general | solution.py:28
  283.1 9.2 %all-to-all-start.4 = ((bf16[32,1,2]{2,1,0:T(2,128)(2,1)}), bf16[32,1,2]{2,1,0:T(2,128)(2,1)S(1)}, u32[]{:S(2)}, u32[]{:S(2)}) async-start(bf16[32,1,2]{2,1,0:T(2,128)(2,1)} %convert_element_type.74), calls=%async_computation.5 | async-start | bytes 32768 | tf_op jit(solution)/shard_map/all_to_all | solution.py:131
  292.3 73.1 %reduce-scatter.2.cloned.1.call-done = bf16[64,7168]{1,0:T(8,128)(2,1)} async-done(((bf16[512,7168]{1,0:T(8,128)(2,1)}), bf16[64,7168]{1,0:T(8,128)(2,1)}) %reduce-scatter.2.cloned.1.call-update) | async-done | bytes 917520 | tf_op jit(solution)/shard_map/reduce_scatter | solution.py:114
  365.4 3.1 convert_element_type.63
  369.1 9.7 %all-to-all-start.3 = ((bf16[32,2,7168]{2,1,0:T(2,128)(2,1)}), bf16[32,2,7168]{2,1,0:T(2,128)(2,1)S(1)}, u32[]{:S(2)}, u32[]{:S(2)}) async-start(bf16[32,2,7168]{2,1,0:T(2,128)(2,1)} %convert_element_type.63), calls=%async_computation.4 | async-start | bytes 1835008 | tf_op jit(solution)/shard_map/all_to_all | solution.py:128
  378.8 5.5 %fusion.2 = bf16[1,128,7168]{2,1,0:T(8,128)(2,1)} fusion(bf16[512,7168]{1,0:T(8,128)(2,1)} %all-gather.3.cloned.1.call-done, f32[512]{0:T(512)S(1)} %convert_element_type.59, f32[512,128]{0,1:T(8,128)S(1)} %fusion.8, f32[512,128]{0,1:T(8,128)S(1)} %fusion.5), kind=kOutput, calls=%fused_computation.11 | convolution fusion | flops 940900352 | bytes 9701376 | tf_op jit(solution)/shard_map/dot_general | solution.py:37
  384.3 6.4 %fusion.1 = bf16[1,7168,128]{2,1,0:T(8,128)(2,1)} fusion(bf16[512,7168]{1,0:T(8,128)(2,1)} %all-gather.5.cloned.1.call-done, bf16[512,128]{0,1:T(8,128)(2,1)S(1)} %get-tuple-element.7), kind=kOutput, calls=%fused_computation.10 | convolution fusion | flops 940441600 | bytes 9306112 | tf_op jit(solution)/shard_map/dot_general | solution.py:34
  390.7 6.5 %fusion = bf16[1,7168,128]{2,1,0:T(8,128)(2,1)} fusion(bf16[512,7168]{1,0:T(8,128)(2,1)} %all-gather.5.cloned.1.call-done, bf16[512,128]{0,1:T(8,128)(2,1)S(1)} %get-tuple-element.8), kind=kOutput, calls=%fused_computation.9 | convolution fusion | flops 940441600 | bytes 9306112 | tf_op jit(solution)/shard_map/dot_general | solution.py:31
  398.8 7.1 %all-to-all-done.3 = bf16[32,2,7168]{2,1,0:T(2,128)(2,1)S(1)} async-done(((bf16[32,2,7168]{2,1,0:T(2,128)(2,1)}), bf16[32,2,7168]{2,1,0:T(2,128)(2,1)S(1)}, u32[]{:S(2)}, u32[]{:S(2)}) %all-to-all-start.3) | async-done | bytes 917536 | tf_op jit(solution)/shard_map/all_to_all | solution.py:128
  407.4 3.1 gather_fusion
  (54 shorter events, 17.9 us)
Async XLA Ops:
  7.2 148.0 %copy-start = (bf16[1,7168,128]{2,1,0:T(8,128)(2,1)S(1)}, bf16[1,7168,128]{2,1,0:T(8,128)(2,1)}, u32[]{:S(2)}) copy-start(bf16[1,7168,128]{2,1,0:T(8,128)(2,1)} %param.11) | copy-start | bytes 5505028
  7.2 148.0 %all-gather.5.cloned.1.call-start = ((), (), s32[]{:S(2)}) async-start(), calls=%async_computation.7 | async-start | bytes 8257536 | tf_op jit(solution)/shard_map/all_gather | solution.py:108
  49.9 3.3 copy-start.4
  53.1 187.1 %all-gather.3.cloned.1.call-start = ((), (), s32[]{:S(2)}) async-start(), calls=%async_computation.6 | async-start | bytes 8257536 | tf_op jit(solution)/shard_map/all_gather | solution.py:109
  100.4 3.2 copy-start.7
  100.4 9.9 %copy-start.8 = (u32[256]{0:T(256)S(1)}, u32[256]{0:T(256)}, u32[]{:S(2)}) copy-start(u32[256]{0:T(256)} %constant.27) | copy-start | bytes 3076
  105.3 14.6 %all-to-all-start = ((bf16[32,1,2]{2,1,0:T(2,128)(2,1)}), bf16[32,1,2]{2,1,0:T(2,128)(2,1)S(1)}, u32[]{:S(2)}, u32[]{:S(2)}) async-start(bf16[32,1,2]{2,1,0:T(2,128)(2,1)} %all_to_all.25), calls=%async_computation | async-start | bytes 32768 | tf_op jit(solution)/shard_map/all_to_all | solution.py:79
  110.0 255.4 %reduce-scatter.2.cloned.1.call-start = ((), (), s32[]{:S(2)}) async-start(), calls=%async_computation.8 | async-start | bytes 8257536 | tf_op jit(solution)/shard_map/reduce_scatter | solution.py:114
  155.2 5.8 %copy-start.1 = (bf16[512,7168]{1,0:T(8,128)(2,1)S(1)}, bf16[512,7168]{1,0:T(8,128)(2,1)}, u32[]{:S(2)}) copy-start(bf16[512,7168]{1,0:T(8,128)(2,1)} %all-gather.5.cloned.1.call-done) | copy-start | bytes 22020100
  155.2 5.8 %copy-start.2 = (bf16[1,7168,128]{2,1,0:T(8,128)(2,1)S(1)}, bf16[1,7168,128]{2,1,0:T(8,128)(2,1)}, u32[]{:S(2)}) copy-start(bf16[1,7168,128]{2,1,0:T(8,128)(2,1)} %param.12) | copy-start | bytes 5505028
  264.0 7.3 %copy-start.3 = (bf16[1,7168,128]{2,1,0:T(8,128)(2,1)S(1)}, bf16[1,7168,128]{2,1,0:T(8,128)(2,1)}, u32[]{:S(2)}) copy-start(bf16[1,7168,128]{2,1,0:T(8,128)(2,1)} %param.12) | copy-start | bytes 5505028
  283.1 85.3 %all-to-all-start.4 = ((bf16[32,1,2]{2,1,0:T(2,128)(2,1)}), bf16[32,1,2]{2,1,0:T(2,128)(2,1)S(1)}, u32[]{:S(2)}, u32[]{:S(2)}) async-start(bf16[32,1,2]{2,1,0:T(2,128)(2,1)} %convert_element_type.74), calls=%async_computation.5 | async-start | bytes 32768 | tf_op jit(solution)/shard_map/all_to_all | solution.py:131
  368.5 0.6 copy-start.5
  369.1 36.8 %all-to-all-start.3 = ((bf16[32,2,7168]{2,1,0:T(2,128)(2,1)}), bf16[32,2,7168]{2,1,0:T(2,128)(2,1)S(1)}, u32[]{:S(2)}, u32[]{:S(2)}) async-start(bf16[32,2,7168]{2,1,0:T(2,128)(2,1)} %convert_element_type.63), calls=%async_computation.4 | async-start | bytes 1835008 | tf_op jit(solution)/shard_map/all_to_all | solution.py:128
  390.7 6.5 %copy-start.6 = (bf16[32,1,2]{2,1,0:T(2,128)(2,1)S(1)}, bf16[32,1,2]{2,1,0:T(2,128)(2,1)}, u32[]{:S(2)}) copy-start(bf16[32,1,2]{2,1,0:T(2,128)(2,1)} %copy-done.5) | copy-start | bytes 388
Sparse Core Ops, SparseCore 0:
  53.2 101.9 all-gather.4
  157.6 82.5 all-gather.2
  281.8 83.5 reduce-scatter.1
where the time goes:
time: 419 us; the launch traced here: 418 us
  waiting for transfers between devices  200 us (48%)
  blocking collectives  95.2 us (23%)
  matrix products  50.5 us (12%)
  local copies, waits for them, and re-layouts  30.8 us (7%)
  starting transfers between devices  23.9 us (6%)
  between operations  15.2 us (4%)
    all_gather x1, waiting for transfers between devices, on_device(): lax.all_gather(rows_dy, 'et', axis=0, tiled=True)  76.6 us
    reduce_scatter x1, waiting for transfers between devices, on_device(): lax.psum_scatter(folded[3].astype(jnp.bfloat16), 'et', scatter_dimension=...  73.1 us
    all_to_all x1, blocking collectives, on_device(): lax.all_to_all(buf_dy, 'exp', split_axis=0, concat_axis=0, tiled=True)  42.3 us
    all_to_all x1, blocking collectives, on_device(): lax.all_to_all(buf_x, 'exp', split_axis=0, concat_axis=0, tiled=True)  35.4 us
    all_gather x1, waiting for transfers between devices, on_device(): lax.all_gather(rows_x, 'et', axis=0, tiled=True)  34.9 us
    unnamed x1, blocking collectives  17.5 us
    dot_general x1, matrix products, expert_terms(): lax.dot_general(grad_up, w_up, (((1,), (1,)), ((), ())), preferred_elemen...  10.3 us
    all_to_all x1, starting transfers between devices, on_device(): lax.all_to_all(part_all.astype(jnp.bfloat16), 'exp', split_axis=0, concat...  9.73 us
  transfers between devices with their start and end apart: 6, of which 5 were waited for; matrix products, arithmetic and copies ran while one was open for 10% of the time, Pallas kernels for 0%

commit v1 on v0

v1 whole, which is shorter than its diff:
```python
import functools
import jax
import jax.numpy as jnp
from jax import lax
from jax.experimental import pallas as pl
from jax.experimental.pallas import tpu as pltpu
from jax.sharding import PartitionSpec as P

TOP = 8
LANE = 128
NS = 6
OCT = 8
MESH = pl.DeviceIdType.MESH
ORDERS = (("x", "y", "z"), ("y", "z", "x"), ("z", "x", "y"))
F32 = jnp.float32
BF16 = jnp.bfloat16


class Torus:
    def __init__(self, nx, ny, nzh, nzl):
        self.n = {"x": nx, "y": ny, "z": nzh * nzl}
        self.nzh, self.nzl = nzh, nzl

    def here(self):
        e = lax.axis_index("exp")
        t = lax.axis_index("et")
        ny, nx = self.n["y"], self.n["x"]
        core = lax.rem(e, 2)
        y = lax.rem(lax.div(e, 2), ny)
        zh = lax.div(e, 2 * ny)
        x = lax.rem(t, nx)
        zl = lax.div(t, nx)
        return {"x": x, "y": y, "z": zh * self.nzl + zl}, core

    def device(self, pos, core):
        zh = lax.div(pos["z"], self.nzl)
        zl = lax.rem(pos["z"], self.nzl)
        return {
            "exp": (zh * self.n["y"] + pos["y"]) * 2 + core,
            "et": zl * self.n["x"] + pos["x"],
        }

    def shift(self, pos, axis, by):
        n = self.n[axis]
        return lax.rem(pos[axis] + (by % n + n), n)

    def neighbour(self, pos, core, axis, by):
        other = dict(pos)
        other[axis] = self.shift(pos, axis, by)
        return self.device(other, core)

    def partners(self, pos, core):
        out = [self.device(pos, 1 - core)]
        for axis in "xyz":
            for d in (1, -1):
                out.append(self.neighbour(pos, core, axis, d))
        return out

    def steps(self, order):
        out = []
        for phase, axis in enumerate(order):
            for k in range(self.n[axis] - 1):
                out.append((phase, k))
        return out

    def weight(self, order, phase, reverse):
        w = 1
        done = order[phase + 1:] if reverse else order[:phase]
        for axis in done:
            w *= self.n[axis]
        return w

    def events(self, orders, reverse):
        out = []
        for s in range(NS):
            order = orders[s // 2]
            at = 0.0
            for i, (phase, k) in enumerate(self.steps(order)):
                at += self.weight(order, phase, reverse) + 0.3
                out.append((at, s, i))
        return [(s, i) for _, s, i in sorted(out)]


def greet(torus, pos, core):
    barrier = pltpu.get_barrier_semaphore()
    partners = torus.partners(pos, core)
    for p in partners:
        pl.semaphore_signal(barrier, inc=1, device_id=p, device_id_type=MESH)
    pl.semaphore_wait(barrier, len(partners))


def cut(torus, ref, width, core, s, at):
    if at.get("z") is None:
        zl, zh = slice(None), slice(None)
    else:
        zl, zh = lax.rem(at["z"], torus.nzl), lax.div(at["z"], torus.nzl)
    y = slice(None) if at.get("y") is None else at["y"]
    if at.get("x") is None:
        col = slice(None)
    else:
        col = pl.ds(pl.multiple_of(at["x"] * width, LANE), width)
    if core is None:
        return ref.at[zl, zh, y, s, :, col]
    return ref.at[zl, zh, y, core, s, :, col]


def gather_kernel(torus, width, blk, out, loc, send, recv, sib_send, sib_recv):
    pos, core = torus.here()
    sibling = torus.device(pos, 1 - core)
    greet(torus, pos, core)
    steps = [torus.steps(ORDERS[s // 2]) for s in range(NS)]

    def region(s, phase, shift):
        order = ORDERS[s // 2]
        at = dict(pos)
        for axis in order[:phase]:
            at[axis] = None
        at[order[phase]] = torus.shift(pos, order[phase], shift)
        return cut(torus, out, width, core, s, at)

    own = [cut(torus, out, width, core, s, pos) for s in range(NS)]

    def ring(s, i):
        phase, k = steps[s][i]
        d = 1 if s % 2 == 0 else -1
        dst = region(s, phase, -d * k)
        src = blk.at[s] if i == 0 else dst
        return pltpu.make_async_remote_copy(
            src_ref=src, dst_ref=dst, send_sem=send.at[s, i], recv_sem=recv.at[s, i],
            device_id=torus.neighbour(pos, core, ORDERS[s // 2][phase], d), device_id_type=MESH)

    def landed(s, i):
        phase, k = steps[s][i]
        d = 1 if s % 2 == 0 else -1
        here = region(s, phase, -d * (k + 1))
        return pltpu.make_async_remote_copy(
            src_ref=here, dst_ref=here, send_sem=send.at[s, i], recv_sem=recv.at[s, i],
            device_id=sibling, device_id_type=MESH), here

    def across(s, src, dst):
        return pltpu.make_async_remote_copy(
            src_ref=src, dst_ref=dst, send_sem=sib_send.at[s], recv_sem=sib_recv.at[s],
            device_id=sibling, device_id_type=MESH)

    for s in range(NS):
        ring(s, 0).start()
    for s in range(NS):
        pltpu.make_async_copy(blk.at[s], own[s], loc.at[s]).start()
        across(s, blk.at[s], own[s]).start()
    for s in range(NS):
        pltpu.make_async_copy(blk.at[s], own[s], loc.at[s]).wait()
    for s, i in torus.events(ORDERS, False):
        arrived, here = landed(s, i)
        arrived.wait_recv()
        if i + 1 < len(steps[s]):
            ring(s, i + 1).start()
        across(s, here, here).start()
    for s in range(NS):
        for i in range(len(steps[s])):
            ring(s, i).wait_send()
        whole = cut(torus, out, width, core, s, {})
        other = cut(torus, out, width, 1 - core, s, {})
        across(s, whole, whole).wait_send()
        across(s, other, other).wait_recv()


def gather_all(torus, blk):
    width = blk.shape[2]
    n = torus.n
    shape = (torus.nzl, torus.nzh, n["y"], 2, NS, OCT, n["x"] * width)
    count = len(torus.steps(ORDERS[0]))
    dma = pltpu.SemaphoreType.DMA
    return pl.pallas_call(
        functools.partial(gather_kernel, torus, width),
        out_shape=jax.ShapeDtypeStruct(shape, blk.dtype),
        in_specs=[pl.BlockSpec(memory_space=pltpu.VMEM)],
        out_specs=pl.BlockSpec(memory_space=pl.ANY),
        scratch_shapes=[dma((NS,)), dma((NS, count)), dma((NS, count)), dma((NS,)), dma((NS,))],
        compiler_params=pltpu.CompilerParams(collective_id=0, has_side_effects=True),
        name="gather_all",
    )(blk)


def back_orders():
    return tuple(tuple(reversed(o)) for o in ORDERS)


def scatter_kernel(torus, width, part, out, mine, theirs, bufs, loc, send, recv, sib_send, sib_recv):
    pos, core = torus.here()
    sibling = torus.device(pos, 1 - core)
    greet(torus, pos, core)
    orders = back_orders()
    steps = [torus.steps(orders[s // 2]) for s in range(NS)]

    def place(s, phase, shift):
        order = orders[s // 2]
        at = dict(pos)
        for axis in order[phase + 1:]:
            at[axis] = None
        at[order[phase]] = torus.shift(pos, order[phase], shift)
        return at

    def slot(s, i):
        phase, k = steps[s][i]
        return bufs[s // 2 * 3 + phase].at[s % 2, k]

    def ring(s, i):
        phase, k = steps[s][i]
        d = 1 if s % 2 == 0 else -1
        src = cut(torus, mine, width, None, s, place(s, phase, -d * (k + 1)))
        return pltpu.make_async_remote_copy(
            src_ref=src, dst_ref=slot(s, i), send_sem=send.at[s, i], recv_sem=recv.at[s, i],
            device_id=torus.neighbour(pos, core, orders[s // 2][phase], d), device_id_type=MESH)

    def add(s, at, buf):
        zs = list(range(torus.n["z"])) if at["z"] is None else None
        ny = torus.n["y"]
        wide = torus.n["x"] * width
        nz = torus.n["z"] if zs else 1
        ys = ny if at["y"] is None else 1
        if at["x"] is None:
            col, cols = pl.ds(0, wide), wide
        else:
            col, cols = pl.ds(pl.multiple_of(at["x"] * width, LANE), width), width

        def one(i, carry):
            iz, iy = lax.div(i, ys), lax.rem(i, ys)
            if at["z"] is None:
                zl, zh = lax.div(iz, torus.nzh), lax.rem(iz, torus.nzh)
                where = (zl, zh)
            else:
                zl, zh = lax.rem(at["z"], torus.nzl), lax.div(at["z"], torus.nzl)
                where = ()
            if at["y"] is None:
                y = iy
                where = where + (iy,)
            else:
                y = at["y"]
            got = buf[where + (slice(None), slice(None))].astype(F32)
            had = mine[zl, zh, y, s, :, col].astype(F32)
            mine[zl, zh, y, s, :, col] = (had + got).astype(BF16)
            return carry

        lax.fori_loop(0, nz * ys, one, 0)

    def fetch(s):
        return pltpu.make_async_copy(
            cut(torus, part, width, core, s, {}), cut(torus, mine, width, None, s, {}), loc.at[s])

    def across(s):
        return pltpu.make_async_remote_copy(
            src_ref=cut(torus, part, width, 1 - core, s, {}), dst_ref=cut(torus, theirs, width, None, s, {}),
            send_sem=sib_send.at[s], recv_sem=sib_recv.at[s], device_id=sibling, device_id_type=MESH)

    for s in range(NS):
        across(s).start()
        fetch(s).start()
    for s in range(NS):
        fetch(s).wait()
        across(s).wait_recv()
        add(s, {"x": None, "y": None, "z": None}, theirs.at[:, :, :, s])
        ring(s, 0).start()
    for s, i in torus.events(orders, True):
        ring(s, i).wait_recv()
        phase, k = steps[s][i]
        d = 1 if s % 2 == 0 else -1
        add(s, place(s, phase, -d * (k + 2)), slot(s, i))
        if i + 1 < len(steps[s]):
            ring(s, i + 1).start()
    zl, zh = lax.rem(pos["z"], torus.nzl), lax.div(pos["z"], torus.nzl)
    for s in range(NS):
        out[s] = mine[zl, zh, pos["y"], s, :, pl.ds(pl.multiple_of(pos["x"] * width, LANE), width)]
    for s in range(NS):
        across(s).wait_send()
        for i in range(len(steps[s])):
            ring(s, i).wait_send()


def scatter_kernel_flat(torus, width, part, out, mine, theirs, b0, b1, b2, b3, b4, b5, b6, b7, b8, *sems):
    scatter_kernel(torus, width, part, out, mine, theirs, (b0, b1, b2, b3, b4, b5, b6, b7, b8), *sems)


def scatter_all(torus, part):
    n = torus.n
    width = part.shape[6] // n["x"]
    half = (torus.nzl, torus.nzh, n["y"], NS, OCT, n["x"] * width)
    orders = back_orders()
    bufs = []
    for order in orders:
        for phase, axis in enumerate(order):
            free = order[phase + 1:]
            shape = (2, n[axis] - 1)
            if "z" in free:
                shape += (torus.nzl, torus.nzh)
            if "y" in free:
                shape += (n["y"],)
            shape += (OCT, n["x"] * width if "x" in free else width)
            bufs.append(pltpu.VMEM(shape, BF16))
    count = len(torus.steps(orders[0]))
    dma = pltpu.SemaphoreType.DMA
    return pl.pallas_call(
        functools.partial(scatter_kernel_flat, torus, width),
        out_shape=jax.ShapeDtypeStruct((NS, OCT, width), BF16),
        in_specs=[pl.BlockSpec(memory_space=pl.ANY)],
        out_specs=pl.BlockSpec(memory_space=pltpu.VMEM),
        scratch_shapes=[pltpu.VMEM(half, BF16), pltpu.VMEM(half, BF16), *bufs,
                        dma((NS,)), dma((NS, count)), dma((NS, count)), dma((NS,)), dma((NS,))],
        compiler_params=pltpu.CompilerParams(
            collective_id=1, has_side_effects=True, vmem_limit_bytes=60 * 1024 * 1024),
        name="scatter_all",
    )(part)


NT = (((1,), (1,)), ((), ()))


def rows_kernel(depth, n_et, x_ref, dy_ref, pick_ref, wg_ref, wu_ref, wd_ref, gt_ref, wt_ref, part_ref, wcat):
    @pl.when(pl.program_id(0) == 0)
    def _():
        wcat[:, :LANE] = wg_ref[...]
        wcat[:, LANE:] = wu_ref[...]

    pre = jnp.dot(x_ref[0, :, :depth], wcat[...], preferred_element_type=F32)
    back = lax.dot_general(dy_ref[0, :, :depth], wd_ref[...], NT, preferred_element_type=F32)
    gate_pre, up_pre = pre[:, :LANE], pre[:, LANE:]
    pick = pick_ref[...]
    scale = jnp.sum(x_ref[0, :, depth:depth + LANE].astype(F32) * pick, axis=1, keepdims=True)
    sigma = jax.nn.sigmoid(gate_pre)
    silu = gate_pre * sigma
    act = silu * up_pre
    score = jnp.sum(act * back, axis=1, keepdims=True)
    dact = scale * back
    grad_gate = dact * up_pre * sigma * (1.0 + gate_pre * (1.0 - sigma))
    grad_up = dact * silu
    both = jnp.concatenate([grad_gate, grad_up], axis=1)
    gt_ref[...] = both.T.astype(BF16)
    wt_ref[...] = (scale * act).T.astype(BF16)
    both = both.astype(BF16)
    cols = depth // n_et
    width = cols + LANE
    for j in range(n_et):
        piece = lax.dot_general(both, wcat[j * cols:(j + 1) * cols, :], NT, preferred_element_type=F32)
        part_ref[j // (n_et // 2), :, (j % (n_et // 2)) * width:(j % (n_et // 2)) * width + cols] = piece.astype(BF16)
        tail = score * pick if j == 0 else jnp.zeros((piece.shape[0], LANE), F32)
        part_ref[j // (n_et // 2), :, (j % (n_et // 2)) * width + cols:(j % (n_et // 2) + 1) * width] = tail.astype(BF16)


def rows_stage(everyone, pick, wg, wu, wd, n_et, tile):
    depth = wg.shape[0]
    rows, wide = everyone.shape[1:]
    out_wide = (depth // n_et + LANE) * (n_et // 2)
    whole = functools.partial(pl.BlockSpec, pipeline_mode=pl.Buffered(1))
    return pl.pallas_call(
        functools.partial(rows_kernel, depth, n_et),
        grid=(rows // tile,),
        in_specs=[
            pl.BlockSpec((1, tile, wide), lambda i: (0, i, 0)),
            pl.BlockSpec((1, tile, wide), lambda i: (1, i, 0)),
            whole((1, LANE), lambda i: (0, 0)),
            whole((depth, LANE), lambda i: (0, 0)),
            whole((depth, LANE), lambda i: (0, 0)),
            whole((LANE, depth), lambda i: (0, 0)),
        ],
        out_specs=[
            pl.BlockSpec((2 * LANE, tile), lambda i: (0, i)),
            pl.BlockSpec((LANE, tile), lambda i: (0, i)),
            pl.BlockSpec((2, tile, out_wide), lambda i: (0, i, 0)),
        ],
        out_shape=[
            jax.ShapeDtypeStruct((2 * LANE, rows), BF16),
            jax.ShapeDtypeStruct((LANE, rows), BF16),
            jax.ShapeDtypeStruct((2, rows, out_wide), BF16),
        ],
        scratch_shapes=[pltpu.VMEM((depth, 2 * LANE), BF16)],
        compiler_params=pltpu.CompilerParams(vmem_limit_bytes=60 * 1024 * 1024),
        name="rows_stage",
    )(everyone, everyone, pick, wg, wu, wd)


def weights_kernel(x_ref, dy_ref, gt_ref, wt_ref, dg_ref, du_ref, dd_ref):
    both = jnp.dot(gt_ref[...], x_ref[0], preferred_element_type=F32).T
    dg_ref[...] = both[:, :LANE].astype(BF16)
    du_ref[...] = both[:, LANE:].astype(BF16)
    dd_ref[...] = jnp.dot(wt_ref[...], dy_ref[0], preferred_element_type=F32).astype(BF16)


def weights_stage(everyone, gt, wt, depth, tile):
    rows = everyone.shape[1]
    return pl.pallas_call(
        weights_kernel,
        grid=(depth // tile,),
        in_specs=[
            pl.BlockSpec((1, rows, tile), lambda i: (0, 0, i)),
            pl.BlockSpec((1, rows, tile), lambda i: (1, 0, i)),
            pl.BlockSpec((2 * LANE, rows), lambda i: (0, 0), pipeline_mode=pl.Buffered(1)),
            pl.BlockSpec((LANE, rows), lambda i: (0, 0), pipeline_mode=pl.Buffered(1)),
        ],
        out_specs=[
            pl.BlockSpec((tile, LANE), lambda i: (i, 0)),
            pl.BlockSpec((tile, LANE), lambda i: (i, 0)),
            pl.BlockSpec((LANE, tile), lambda i: (0, i)),
        ],
        out_shape=[
            jax.ShapeDtypeStruct((depth, LANE), BF16),
            jax.ShapeDtypeStruct((depth, LANE), BF16),
            jax.ShapeDtypeStruct((LANE, depth), BF16),
        ],
        compiler_params=pltpu.CompilerParams(vmem_limit_bytes=60 * 1024 * 1024),
        name="weights_stage",
    )(everyone, everyone, gt, wt)


def on_device(torus, tokens, grad_out, gates, expert_ids, gate_weight, up_weight, down_weight):
    count, depth = tokens.shape
    n_exp = lax.axis_size("exp")
    n_et = lax.axis_size("et")
    experts = jnp.arange(LANE, dtype=jnp.int32)
    chosen = expert_ids[:, :, None] == experts[None, None, :]
    table = jnp.sum(jnp.where(chosen, gates[:, :, None].astype(F32), 0.0), axis=1).astype(BF16)
    half = -(-(depth + LANE) // (n_et // 2 * LANE)) * (n_et // 2 * LANE)
    packed = jnp.concatenate([
        tokens, table, jnp.zeros((count, half - depth - LANE), BF16),
        grad_out, jnp.zeros((count, half - depth), BF16)], axis=1)
    blk = lax.all_to_all(packed, "et", split_axis=1, concat_axis=0, tiled=True)
    blk = blk.reshape(NS, OCT, blk.shape[1])
    everyone = gather_all(torus, blk)
    rows = n_exp * n_et * count
    everyone = everyone.reshape(2, rows, half)
    pick = (experts == lax.axis_index("exp")).astype(F32)[None, :]
    wg, wu, wd = gate_weight[0], up_weight[0], down_weight[0]
    gt, wt, part = rows_stage(everyone, pick, wg, wu, wd, n_et, 256 if rows % 256 == 0 else 128)
    part = part.reshape(torus.nzl, torus.nzh, torus.n["y"], 2, NS, OCT, part.shape[2])
    mine = scatter_all(torus, part)
    mine = mine.reshape(NS * OCT, mine.shape[2])
    owned = lax.all_to_all(mine, "et", split_axis=0, concat_axis=1, tiled=True)
    owned = owned.reshape(count, n_et, owned.shape[1] // n_et)
    cols = depth // n_et
    input_grad = owned[:, :, :cols].reshape(count, depth)
    scores = owned[:, 0, cols:].astype(F32)
    gate_grad = jnp.sum(jnp.where(chosen, scores[:, None, :], 0.0), axis=2)
    dg, du, dd = weights_stage(everyone, gt, wt, depth, min(512, depth))
    return input_grad, gate_grad, dg[None], du[None], dd[None]


def solution(mesh, dims=(4, 4, 4, 2)):
    placed = (
        P(("exp", "et"), None),
        P(("exp", "et"), None),
        P(("exp", "et"), None),
        P(("exp", "et"), None),
        P("exp", None, "et"),
        P("exp", None, "et"),
        P("exp", "et", None),
    )
    return jax.shard_map(
        functools.partial(on_device, Torus(*dims)),
        mesh=mesh,
        in_specs=placed,
        out_specs=(
            P(("exp", "et"), None),
            P(("exp", "et"), None),
            P("exp", None, "et"),
            P("exp", None, "et"),
            P("exp", "et", None),
        ),
        check_vma=False,
    )
```

time: 419 us -> 334 us (0.80)
  Pallas kernels: 0 us -> 306 us
  waiting for transfers between devices: 200 us -> 5.23 us
  blocking collectives: 95.2 us -> 0 us
  matrix products: 50.5 us -> 0 us
  local copies, waits for them, and re-layouts: 30.8 us -> 7.85 us
  between operations: 15.2 us -> 0.66 us
  starting transfers between devices: 23.9 us -> 10.3 us
    pallas_call x0 -> x4, Pallas kernels: none -> 306 us  [the longest x1 140 us: gather_all(): pl.pallas_call(functools.partial(gather_kernel, torus, width), out_shape=...]
    all_gather x2 -> x0, waiting for transfers between devices: 112 us -> none  [the longest x1 76.6 us: on_device(): lax.all_gather(rows_dy, 'et', axis=0, tiled=True)]
    all_to_all x2 -> x0, blocking collectives: 77.7 us -> none  [the longest x1 42.3 us: on_device(): lax.all_to_all(buf_dy, 'exp', split_axis=0, concat_axis=0, tiled=True)]
    reduce_scatter x1 -> x0, waiting for transfers between devices: 73.1 us -> none  [on_device(): lax.psum_scatter(folded[3].astype(jnp.bfloat16), 'et', scatter_dimension=...]
    dot_general x8 -> x0, matrix products: 50.5 us -> none  [the longest x1 10.3 us: expert_terms(): lax.dot_general(grad_up, w_up, (((1,), (1,)), ((), ())), preferred_elemen...]
    unnamed x1 -> x0, blocking collectives: 17.5 us -> none
    all_to_all x3 -> x2, starting transfers between devices: 23.6 us -> 10.3 us  [the longest x1 5.76 us: on_device(): blk = lax.all_to_all(packed, 'et', split_axis=1, concat_axis=0, tiled=True)]
    all_to_all x3 -> x2, waiting for transfers between devices: 15.5 us -> 5.23 us  [the longest x1 5.22 us: on_device(): blk = lax.all_to_all(packed, 'et', split_axis=1, concat_axis=0, tiled=True)]
  transfers between devices with their start and end apart: 6 -> 2, of which waited for: 5 -> 1; matrix products, arithmetic and copies ran while one was open for 10% -> 0% of each run, Pallas kernels for 0% -> 7%
where the time goes in v1:
time: 334 us; the launch traced here: 333 us
  Pallas kernels  306 us (92%)
  starting transfers between devices  10.3 us (3%)
  local copies, waits for them, and re-layouts  7.85 us (2%)
  waiting for transfers between devices  5.23 us (2%)
    pallas_call x1, Pallas kernels, gather_all(): pl.pallas_call(functools.partial(gather_kernel, torus, width), out_shape=...  140 us
    pallas_call x1, Pallas kernels, scatter_all(): pl.pallas_call(functools.partial(scatter_kernel_flat, torus, width), out_...  110 us
    pallas_call x1, Pallas kernels, rows_stage(): pl.pallas_call(functools.partial(rows_kernel, depth, n_et), grid=(rows //...  33.3 us
    pallas_call x1, Pallas kernels, weights_stage(): pl.pallas_call(weights_kernel, grid=(depth // tile,), in_specs=[pl.BlockS...  22.3 us
  transfers between devices with their start and end apart: 2, of which 1 were waited for; matrix products, arithmetic and copies ran while one was open for 0% of the time, Pallas kernels for 7%

profile of v1, /device:TPU:32, one launch (start us, length us, event | category | flops | bytes accessed | tf_op | source)
XLA Modules:
  0.0 333.0 jit_solution(17220908110747068787)
XLA Ops:
  0.6 1.6 constant_dynamic-update-slice_fusion.4
  2.2 0.7 convert_element_type.19
  2.9 0.8 select_reduce_fusion.1
  3.6 0.6 constant_dynamic-update-slice_fusion.3
  4.2 0.6 constant_dynamic-update-slice_fusion.2
  4.8 1.6 constant_dynamic-update-slice_fusion.1
  6.4 0.6 constant_dynamic-update-slice_fusion
  7.0 5.8 %all-to-all-start = ((bf16[6,8,1920]{2,0,1:T(8,128)(2,1)}), bf16[6,8,1920]{2,0,1:T(8,128)(2,1)S(1)}, u32[]{:S(2)}, u32[]{:S(2)}) async-start(bf16[6,8,1920]{2,0,1:T(8,128)(2,1)} %bitcast), calls=%async_computation | async-start | bytes 491520 | tf_op jit(solution)/shard_map/all_to_all | solution.py:424
  12.7 0.5 compare_convert_fusion.pick_ref
  13.2 5.2 %all-to-all-done = bf16[6,8,1920]{2,0,1:T(8,128)(2,1)S(1)} async-done(((bf16[6,8,1920]{2,0,1:T(8,128)(2,1)}), bf16[6,8,1920]{2,0,1:T(8,128)(2,1)S(1)}, u32[]{:S(2)}, u32[]{:S(2)}) %all-to-all-start) | async-done | bytes 184352 | tf_op jit(solution)/shard_map/all_to_all | solution.py:424
  18.5 0.7 reshape.46.blk
  19.2 140.4 %gather_all.1 = bf16[2,4,4,2,6,8,7680]{6,5,4,3,2,1,0:T(8,128)(2,1)} custom-call(bf16[6,8,1920]{2,1,0:T(8,128)(2,1)} %reshape.46.blk), custom_call_target="tpu_custom_call" | custom-call | tf_op jit(solution)/shard_map/gather_all/pallas_call | solution.py:173
  159.6 33.3 %rows_stage.1 = (bf16[256,1536]{1,0:T(8,128)(2,1)}, bf16[128,1536]{1,0:T(8,128)(2,1)}, bf16[2,1536,4096]{2,1,0:T(8,128)(2,1)}) custom-call(bf16[2,1536,7680]{2,1,0:T(8,128)(2,1)} %bitcast.17, bf16[2,1536,7680]{2,1,0:T(8,128)(2,1)} %bitcast.18, f32[1,128]{1,0:T(1,128)} %compare_convert_fusion.pick_ref, bf16[7168,128]{1,0:T(8,128)(2,1)} %bitcast.22, ...), custom_call_target="tpu_custom_call" | custom-call | tf_op jit(solution)/shard_map/rows_stage/pallas_call | solution.py:353
  192.9 110.3 %scatter_all.1 = bf16[6,8,1024]{2,1,0:T(8,128)(2,1)} custom-call(bf16[2,4,4,2,6,8,4096]{6,5,4,3,2,1,0:T(8,128)(2,1)} %bitcast.21), custom_call_target="tpu_custom_call" | custom-call | tf_op jit(solution)/shard_map/scatter_all/pallas_call | solution.py:301
  303.2 1.6 all_to_all.27
  304.8 4.5 %all-to-all-start.1 = ((bf16[8,6,1024]{2,1,0:T(8,128)(2,1)}), bf16[8,6,1024]{2,1,0:T(8,128)(2,1)S(1)}, u32[]{:S(2)}, u32[]{:S(2)}) async-start(bf16[8,6,1024]{2,1,0:T(8,128)(2,1)} %all_to_all.27), calls=%async_computation.1 | async-start | bytes 262144 | tf_op jit(solution)/shard_map/all_to_all | solution.py:435
  309.3 0.0 copy-start
  309.3 22.3 %weights_stage.1 = (bf16[7168,128]{1,0:T(8,128)(2,1)}, bf16[7168,128]{1,0:T(8,128)(2,1)}, bf16[128,7168]{1,0:T(8,128)(2,1)}) custom-call(bf16[2,1536,7680]{2,1,0:T(8,128)(2,1)} %bitcast.19, bf16[2,1536,7680]{2,1,0:T(8,128)(2,1)} %bitcast.20, bf16[256,1536]{1,0:T(8,128)(2,1)} %get-tuple-element.12.gt_ref, bf16[128,1536]{1,0:T(8,128)(2,1)} %get-tuple-element.13.wt_ref), custom_call_target="tpu_custom_call" | custom-call | tf_op jit(solution)/shard_map/weights_stage/pallas_call | solution.py:389
  331.6 0.0 all-to-all-done.1
  331.6 0.7 slice.8
  332.3 0.0 copy-done
  332.3 0.7 select_reduce_fusion
  (1 shorter events, 0.0 us)
Async XLA Ops:
  7.0 11.5 %all-to-all-start = ((bf16[6,8,1920]{2,0,1:T(8,128)(2,1)}), bf16[6,8,1920]{2,0,1:T(8,128)(2,1)S(1)}, u32[]{:S(2)}, u32[]{:S(2)}) async-start(bf16[6,8,1920]{2,0,1:T(8,128)(2,1)} %bitcast), calls=%async_computation | async-start | bytes 491520 | tf_op jit(solution)/shard_map/all_to_all | solution.py:424
  304.8 26.9 %all-to-all-start.1 = ((bf16[8,6,1024]{2,1,0:T(8,128)(2,1)}), bf16[8,6,1024]{2,1,0:T(8,128)(2,1)S(1)}, u32[]{:S(2)}, u32[]{:S(2)}) async-start(bf16[8,6,1024]{2,1,0:T(8,128)(2,1)} %all_to_all.27), calls=%async_computation.1 | async-start | bytes 262144 | tf_op jit(solution)/shard_map/all_to_all | solution.py:435
  309.3 23.0 %copy-start = (s32[6,8]{1,0:T(8,128)S(1)}, s32[6,8]{1,0:T(8,128)}, u32[]{:S(2)}) copy-start(s32[6,8]{1,0:T(8,128)} %param.10) | copy-start | bytes 580

commit v2 on v0

v2 whole, which is shorter than its diff:
```python
import functools
import jax
import jax.numpy as jnp
from jax import lax
from jax.experimental import pallas as pl
from jax.experimental.pallas import tpu as pltpu
from jax.sharding import PartitionSpec as P

TOP = 8
LANE = 128
NS = 6
OCT = 8
MESH = pl.DeviceIdType.MESH
ORDERS = (("x", "y", "z"), ("z", "y", "x"), ("z", "x", "y"))
ROWS = 16
NT = (((1,), (1,)), ((), ()))
F32 = jnp.float32
BF16 = jnp.bfloat16


class Torus:
    def __init__(self, nx, ny, nzh, nzl):
        self.n = {"x": nx, "y": ny, "z": nzh * nzl}
        self.nzh, self.nzl = nzh, nzl

    def here(self):
        e = lax.axis_index("exp")
        t = lax.axis_index("et")
        ny, nx = self.n["y"], self.n["x"]
        core = lax.rem(e, 2)
        y = lax.rem(lax.div(e, 2), ny)
        zh = lax.div(e, 2 * ny)
        x = lax.rem(t, nx)
        zl = lax.div(t, nx)
        return {"x": x, "y": y, "z": zh * self.nzl + zl}, core

    def split(self, z):
        return lax.rem(z, self.nzl), lax.div(z, self.nzl)

    def device(self, pos, core):
        zl, zh = self.split(pos["z"])
        return {
            "exp": (zh * self.n["y"] + pos["y"]) * 2 + core,
            "et": zl * self.n["x"] + pos["x"],
        }

    def shift(self, pos, axis, by):
        n = self.n[axis]
        return lax.rem(pos[axis] + (by % n + n), n)

    def moved(self, pos, axis, by):
        other = dict(pos)
        other[axis] = self.shift(pos, axis, by)
        return other

    def experts(self):
        return [(c, y, h) for c in range(2) for y in range(self.n["y"]) for h in range(self.nzh) if c or y or h]

    def other_expert(self, pos, core, offset, sign):
        c, y, h = offset
        out = self.moved(pos, "y", sign * y)
        out["z"] = self.shift(pos, "z", sign * h * self.nzl)
        return out, (1 - core if c else core)

    def greet(self, pos, core):
        seen, partners = set(), []
        for c, y, h in self.experts():
            p, k = self.other_expert(pos, core, (c, y, h), 1)
            partners.append(self.device(p, k))
            if not c and not y:
                seen.add(("z", h * self.nzl))
            if not c and not h:
                seen.add(("y", y))
        for axis in "xyz":
            for by in range(1, self.n[axis]):
                if (axis, by) not in seen:
                    partners.append(self.device(self.moved(pos, axis, by), core))
        barrier = pltpu.get_barrier_semaphore()
        for p in partners:
            pl.semaphore_signal(barrier, inc=1, device_id=p, device_id_type=MESH)
        pl.semaphore_wait(barrier, len(partners))


def remote(src, dst, send, recv, device):
    return pltpu.make_async_remote_copy(
        src_ref=src, dst_ref=dst, send_sem=send, recv_sem=recv, device_id=device, device_id_type=MESH)


def chosen_part(torus, at, part, width):
    zl, zh, y = slice(None), slice(None), slice(None)
    if at["z"] is not None:
        zl, zh = torus.split(at["z"])
    if at["y"] is not None:
        y = at["y"]
    col = slice(None)
    if at["x"] is not None:
        col = pl.ds(pl.multiple_of(at["x"] * width, LANE), width)
    if part is not None:
        if at["z"] is None:
            zl = part
        elif at["y"] is None:
            n = torus.n["y"] // 2
            y = pl.ds(part * n, n)
        else:
            n = torus.n["x"] // 2 * width
            col = pl.ds(part * n, n)
    return zl, zh, y, col


def volume(torus, axes):
    w = 1
    for a in axes:
        w *= torus.n[a]
    return w


def gather_kernel(torus, width, blk, sel, out, gate_out, gate_in, loc, p1_send, p1_recv, send, recv, sib_send,
                  sib_recv, g_send, g_recv):
    pos, core = torus.here()
    me = torus.device(pos, core)["exp"]
    sibling = torus.device(pos, 1 - core)
    torus.greet(pos, core)

    def region(s, phase, shift, part=None, c=core):
        order = ORDERS[s // 2]
        at = dict(pos)
        for axis in order[:phase]:
            at[axis] = None
        if phase < 3:
            at[order[phase]] = torus.shift(pos, order[phase], shift)
        zl, zh, y, col = chosen_part(torus, at, part, width)
        return out.at[zl, s % 2, zh, y, c, s // 2, :, col]

    def first(s, by):
        axis = ORDERS[s // 2][0]
        return remote(blk.at[s % 2, s // 2], region(s, 0, 0), p1_send.at[s, by - 1], p1_recv.at[s, by - 1],
                      torus.device(torus.moved(pos, axis, by), core))

    def first_landed(s, by):
        here = region(s, 0, -by)
        return remote(here, here, p1_send.at[s, by - 1], p1_recv.at[s, by - 1], sibling)

    def ring(s, phase, k, part):
        d = 1 if s % 2 == 0 else -1
        here = region(s, phase, -d * k, part)
        i = phase - 1
        return remote(here, here, send.at[s, i, k, part], recv.at[s, i, k, part],
                      torus.device(torus.moved(pos, ORDERS[s // 2][phase], d), core))

    def landed(s, phase, k, part):
        d = 1 if s % 2 == 0 else -1
        here = region(s, phase, -d * (k + 1), part)
        return remote(here, here, send.at[s, phase - 1, k, part], recv.at[s, phase - 1, k, part], sibling)

    def across(s, src, dst):
        return remote(src, dst, sib_send.at[s], sib_recv.at[s], sibling)

    def own(s):
        return pltpu.make_async_copy(blk.at[s % 2, s // 2], region(s, 0, 0), loc.at[s])

    for s in range(NS):
        for by in range(1, torus.n[ORDERS[s // 2][0]]):
            first(s, by).start()
        own(s).start()
    for q, offset in enumerate(torus.experts()):
        p, k = torus.other_expert(pos, core, offset, 1)
        to = torus.device(p, k)
        remote(sel.at[to["exp"]], gate_in.at[me], g_send.at[q], g_recv.at[q], to).start()
    gate_in[me] = sel[me]
    for s in range(NS):
        own(s).wait()
        for by in range(1, torus.n[ORDERS[s // 2][0]]):
            first_landed(s, by).wait_recv()
        for part in range(2):
            ring(s, 1, 0, part).start()
        whole = region(s, 1, 0)
        across(s, whole, whole).start()
    events = []
    for s in range(NS):
        order = ORDERS[s // 2]
        at = 0.0
        for phase in (1, 2):
            w = volume(torus, order[:phase]) * (1.5 if phase == 1 else 1.0)
            for k in range(torus.n[order[phase]] - 1):
                for part in range(2):
                    at += w / 2 + 0.5
                    events.append((at, s, phase, k, part))
            at += 1.0
    for _, s, phase, k, part in sorted(events):
        order = ORDERS[s // 2]
        arrived = landed(s, phase, k, part)
        arrived.wait_recv()
        if k + 1 < torus.n[order[phase]] - 1:
            ring(s, phase, k + 1, part).start()
        elif phase == 1 and part == 1:
            for half in range(2):
                ring(s, 2, 0, half).start()
        d = 1 if s % 2 == 0 else -1
        here = region(s, phase, -d * (k + 1), part)
        across(s, here, here).start()
    for q, offset in enumerate(torus.experts()):
        p, k = torus.other_expert(pos, core, offset, -1)
        came = torus.device(p, k)
        remote(sel.at[me], gate_in.at[came["exp"]], g_send.at[q], g_recv.at[q], came).wait_recv()
    gate_out[...] = gate_in[...]
    for s in range(NS):
        order = ORDERS[s // 2]
        for by in range(1, torus.n[order[0]]):
            first(s, by).wait_send()
        for phase in (1, 2):
            for k in range(torus.n[order[phase]] - 1):
                for part in range(2):
                    ring(s, phase, k, part).wait_send()
        whole, other = region(s, 3, 0), region(s, 3, 0, None, 1 - core)
        across(s, whole, whole).wait_send()
        across(s, other, other).wait_recv()
    for q, offset in enumerate(torus.experts()):
        p, k = torus.other_expert(pos, core, offset, 1)
        to = torus.device(p, k)
        remote(sel.at[to["exp"]], gate_in.at[me], g_send.at[q], g_recv.at[q], to).wait_send()


def gather_all(torus, blk, sel):
    width = blk.shape[3]
    n = torus.n
    shape = (torus.nzl, 2, torus.nzh, n["y"], 2, NS // 2, ROWS, n["x"] * width)
    most = max(n.values()) - 1
    others = len(torus.experts())
    dma = pltpu.SemaphoreType.DMA
    return pl.pallas_call(
        functools.partial(gather_kernel, torus, width),
        out_shape=[jax.ShapeDtypeStruct(shape, blk.dtype), jax.ShapeDtypeStruct(sel.shape, sel.dtype)],
        in_specs=[pl.BlockSpec(memory_space=pltpu.VMEM)] * 2,
        out_specs=[pl.BlockSpec(memory_space=pl.ANY), pl.BlockSpec(memory_space=pltpu.VMEM)],
        scratch_shapes=[pltpu.VMEM(sel.shape, sel.dtype), dma((NS,)), dma((NS, most)), dma((NS, most)),
                        dma((NS, 2, most, 2)), dma((NS, 2, most, 2)), dma((NS,)), dma((NS,)),
                        dma((others,)), dma((others,))],
        compiler_params=pltpu.CompilerParams(collective_id=0, has_side_effects=True),
        name="gather_all",
    )(blk, sel)


BACK = tuple(tuple(reversed(o)) for o in ORDERS)


def back_kernel(torus, depth, tile_cols, every, gates, wg, wu, wd, out, score_out, dg, du, dd,
                part, theirs, wcat, wdown, gt, wt, score, score_in, b0, b1, b2, b3, b4, b5, b6, b7, b8,
                w_sem, sib_send, sib_recv, send, recv, p3_send, p3_recv, s_send, s_recv):
    bufs = (b0, b1, b2, b3, b4, b5, b6, b7, b8)
    n = torus.n
    width = depth // (torus.nzl * n["x"])
    wide = n["x"] * width
    pos, core = torus.here()
    me = torus.device(pos, core)["exp"]
    sibling = torus.device(pos, 1 - core)
    hz = torus.nzh // 2
    group = hz * n["y"] * 2
    rows = group * ROWS
    tiles = NS
    half = depth // 2

    loads = [pltpu.make_async_copy(wg, wcat.at[:, pl.ds(0, LANE)], w_sem.at[0]),
             pltpu.make_async_copy(wu, wcat.at[:, pl.ds(LANE, LANE)], w_sem.at[1]),
             pltpu.make_async_copy(wd, wdown, w_sem.at[2])]
    for c in loads:
        c.start()

    def block(at, s, k=core):
        zl, zh, y, col = chosen_part(torus, at, None, width)
        return part.at[k, zl, zh, y, s, :, col]

    def place(s, phase, shift):
        order = BACK[s // 2]
        at = dict(pos)
        for axis in order[phase + 1:]:
            at[axis] = None
        at[order[phase]] = torus.shift(pos, order[phase], shift)
        return at

    def piece(at, s, h):
        zl, zh, y, col = chosen_part(torus, at, h, width)
        return part.at[core, zl, zh, y, s, :, col]

    def slot(s, phase, k, h):
        ref = bufs[s // 2 * 3 + phase].at[s % 2, k]
        if h is None:
            return ref
        order = BACK[s // 2]
        if "z" in order[phase + 1:]:
            return ref.at[h]
        if "y" in order[phase + 1:]:
            return ref.at[pl.ds(h * (n["y"] // 2), n["y"] // 2)]
        return ref.at[:, pl.ds(h * (n["x"] // 2) * width, n["x"] // 2 * width)]

    def ring(s, phase, k, h):
        d = 1 if s % 2 == 0 else -1
        return remote(piece(place(s, phase, -d * (k + 1)), s, h), slot(s, phase, k, h),
                      send.at[s, phase, k, h], recv.at[s, phase, k, h],
                      torus.device(torus.moved(pos, BACK[s // 2][phase], d), core))

    def last(s, by):
        axis = BACK[s // 2][2]
        return remote(block(place(s, 2, by), s), bufs[s // 2 * 3 + 2].at[s % 2, by - 1],
                      p3_send.at[s, by - 1], p3_recv.at[s, by - 1],
                      torus.device(torus.moved(pos, axis, by), core))

    def add(s, at, got, h):
        zl0, zh0, y0, col0 = None, None, None, None
        nzl, nzh, ny = 1, 1, 1
        zbase = ybase = 0
        if at["z"] is None:
            nzh = torus.nzh
            nzl = torus.nzl if h is None else 1
            zbase = 0 if h is None else h
        else:
            zl0, zh0 = torus.split(at["z"])
        if at["y"] is None:
            ny = n["y"]
            if h is not None and at["z"] is not None:
                ny, ybase = n["y"] // 2, h * (n["y"] // 2)
        else:
            y0 = at["y"]
        if at["x"] is None:
            cols = wide
            col0 = pl.ds(0, wide)
            if h is not None and at["z"] is not None and at["y"] is not None:
                cols = wide // 2
                col0 = pl.ds(h * cols, cols)
        else:
            cols = width
            col0 = pl.ds(pl.multiple_of(at["x"] * width, LANE), width)

        def one(i, carry):
            iy = lax.rem(i, ny)
            iz = lax.div(i, ny)
            izh = lax.rem(iz, nzh)
            izl = lax.div(iz, nzh)
            where = ()
            if at["z"] is None:
                where = (izh,) if h is not None else (izl, izh)
                zl, zh = izl + zbase, izh
            else:
                zl, zh = zl0, zh0
            if at["y"] is None:
                where = where + (iy,)
                y = iy + ybase
            else:
                y = y0
            g = got[where + (slice(None), slice(None))].astype(F32)
            p = part[core, zl, zh, y, s, :, col0].astype(F32)
            part[core, zl, zh, y, s, :, col0] = (p + g).astype(BF16)
            return carry

        lax.fori_loop(0, nzl * nzh * ny, one, 0)

    def cross(t):
        o, hh = t // 2, t % 2
        zs, os = pl.ds(hh * hz, hz), pl.ds(2 * o, 2)
        return remote(part.at[1 - core, :, zs, :, os], theirs.at[:, zs, :, os], sib_send.at[t], sib_recv.at[t], sibling)

    everywhere = {"x": None, "y": None, "z": None}

    def begin(o):
        for t in (2 * o, 2 * o + 1):
            cross(t).wait_recv()
        for s in (2 * o, 2 * o + 1):
            add(s, everywhere, theirs.at[:, :, :, s], None)
            for h in range(2):
                ring(s, 0, 0, h).start()

    def rows_phase(xs, ds, x_sem, d_sem):
        def fetch(which, t):
            o, hh = t // 2, t % 2
            buf, sem = (xs, x_sem) if which == 0 else (ds, d_sem)
            return [pltpu.make_async_copy(every.at[which, d, pl.ds(hh * hz, hz), :, :, o], buf.at[d], sem.at[d])
                    for d in range(2)]

        for which in range(2):
            for c in fetch(which, 0):
                c.start()
        score[...] = jnp.zeros_like(score)
        torus.greet(pos, core)
        for c in loads:
            c.wait()
        for t in range(tiles):
            o, hh = t // 2, t % 2
            for c in fetch(0, t):
                c.wait()
            pre = jnp.dot(xs[0].reshape(rows, half), wcat[:half, :], preferred_element_type=F32)
            pre = pre + jnp.dot(xs[1].reshape(rows, half), wcat[half:, :], preferred_element_type=F32)
            if t + 1 < tiles:
                for c in fetch(0, t + 1):
                    c.start()
            for c in fetch(1, t):
                c.wait()
            back = lax.dot_general(ds[0].reshape(rows, half), wdown[:, :half], NT, preferred_element_type=F32)
            back = back + lax.dot_general(ds[1].reshape(rows, half), wdown[:, half:], NT, preferred_element_type=F32)
            if t + 1 < tiles:
                for c in fetch(1, t + 1):
                    c.start()
            gate_pre, up_pre = pre[:, :LANE], pre[:, LANE:]
            scale = gates[t]
            sigma = jax.nn.sigmoid(gate_pre)
            silu = gate_pre * sigma
            act = silu * up_pre
            dact = scale * back
            grad_gate = dact * up_pre * sigma * (1.0 + gate_pre * (1.0 - sigma))
            grad_up = dact * silu
            cols = pl.ds(t * rows, rows)
            gt[:LANE, cols] = grad_gate.T.astype(BF16)
            gt[LANE:, cols] = grad_up.T.astype(BF16)
            wt[:, cols] = (scale * act).T.astype(BF16)
            sums = jnp.sum((act * back).T, axis=0, keepdims=True)
            each = rows // hz
            for z in range(hz):
                score[hh * hz + z, o:o + 1, :each] = sums[:, z * each:(z + 1) * each]
            both = jnp.concatenate([grad_gate.astype(BF16), grad_up.astype(BF16)], axis=1)
            for j in range(torus.nzl * n["x"]):
                zl, x = j // n["x"], j % n["x"]
                grad = lax.dot_general(both, wcat[j * width:(j + 1) * width, :], NT, preferred_element_type=F32)
                grad = grad.reshape(hz, n["y"], 2, 2, OCT, width).astype(BF16)
                for k in range(2):
                    part[k, zl, hh * hz:(hh + 1) * hz, :, 2 * o:2 * o + 2, :, x * width:(x + 1) * width] = grad[:, :, k]
            cross(t).start()
            if t in (2, 4):
                begin(t // 2 - 1)

    pl.run_scoped(
        rows_phase,
        pltpu.VMEM((2, hz, n["y"], 2, ROWS, half), BF16), pltpu.VMEM((2, hz, n["y"], 2, ROWS, half), BF16),
        pltpu.SemaphoreType.DMA((2,)), pltpu.SemaphoreType.DMA((2,)))

    def message(q, offset, sign):
        p, k = torus.other_expert(pos, core, offset, sign)
        other = torus.device(p, k)
        zh = torus.split(p["z"])[1]
        mine = score.at[zh] if sign > 0 else score.at[0]
        return remote(mine, score_in.at[me if sign > 0 else other["exp"]], s_send.at[q], s_recv.at[q], other)

    for q, offset in enumerate(torus.experts()):
        message(q, offset, 1).start()
    score_in[me] = score[torus.split(pos["z"])[1]]

    def exchange(xt, dt, sg, su, sd, x_sem, d_sem, o_sem):
        units = depth // tile_cols
        per = half // tile_cols

        def fetch(u, which):
            buf, sem = (xt, x_sem) if which == 0 else (dt, d_sem)
            d, c = u // per, pl.ds(u % per * tile_cols, tile_cols)
            return [pltpu.make_async_copy(every.at[which, d, pl.ds(t % 2 * hz, hz), :, :, t // 2, :, c],
                                          buf.at[u % 2, t], sem.at[u % 2, t]) for t in range(tiles)]

        def put(u):
            c = pl.ds(u * tile_cols, tile_cols)
            return [pltpu.make_async_copy(sg.at[u % 2], dg.at[c], o_sem.at[u % 2, 0]),
                    pltpu.make_async_copy(su.at[u % 2], du.at[c], o_sem.at[u % 2, 1]),
                    pltpu.make_async_copy(sd.at[u % 2], dd.at[:, c], o_sem.at[u % 2, 2])]

        def get(u):
            for which in range(2):
                for c in fetch(u, which):
                    c.start()

        def unit(u):
            if u + 1 < units:
                get(u + 1)
            for which in range(2):
                for c in fetch(u, which):
                    c.wait()
            if u >= 2:
                for c in put(u - 2):
                    c.wait()
            both = jnp.dot(gt[...], xt[u % 2].reshape(tiles * rows, tile_cols), preferred_element_type=F32).T
            sg[u % 2] = both[:, :LANE].astype(BF16)
            su[u % 2] = both[:, LANE:].astype(BF16)
            down = jnp.dot(wt[...], dt[u % 2].reshape(tiles * rows, tile_cols), preferred_element_type=F32)
            sd[u % 2] = down.astype(BF16)
            for c in put(u):
                c.start()

        get(0)
        begin(2)
        events = []
        for s in range(NS):
            order = BACK[s // 2]
            at = (s // 2) * 3.0
            for phase in (0, 1):
                w = volume(torus, order[phase + 1:])
                for k in range(n[order[phase]] - 1):
                    for h in range(2):
                        at += w / 2 + 0.5
                        events.append((at, s, phase, k, h))
                at += 2.0
            events.append((at + 6.0, s, 2, 0, 0))
        events.sort()
        done = 0
        for i, (_, s, phase, k, h) in enumerate(events):
            while done < units and done * len(events) * 3 // 5 <= i * units:
                unit(done)
                done += 1
            order = BACK[s // 2]
            d = 1 if s % 2 == 0 else -1
            if phase < 2:
                ring(s, phase, k, h).wait_recv()
                add(s, place(s, phase, -d * (k + 2)), slot(s, phase, k, h), h)
                if k + 1 < n[order[phase]] - 1:
                    ring(s, phase, k + 1, h).start()
                elif h == 1 and phase == 0:
                    for hh in range(2):
                        ring(s, 1, 0, hh).start()
                elif h == 1:
                    for by in range(1, n[order[2]]):
                        last(s, by).start()
            else:
                zl, zh = torus.split(pos["z"])
                col = pl.ds(pl.multiple_of(pos["x"] * width, LANE), width)
                total = part[core, zl, zh, pos["y"], s, :, col].astype(F32)
                for by in range(1, n[order[2]]):
                    last(s, by).wait_recv()
                    total = total + bufs[s // 2 * 3 + 2][s % 2, by - 1].astype(F32)
                out[s] = total.astype(BF16)
        while done < units:
            unit(done)
            done += 1
        for u in (units - 2, units - 1):
            for c in put(u):
                c.wait()

    stage = pltpu.VMEM((2, tile_cols, LANE), BF16)
    tiled = pltpu.VMEM((2, tiles, hz, n["y"], 2, ROWS, tile_cols), BF16)
    dma = pltpu.SemaphoreType.DMA
    pl.run_scoped(exchange, tiled, tiled, stage, stage, pltpu.VMEM((2, LANE, tile_cols), BF16),
                  dma((2, tiles)), dma((2, tiles)), dma((2, 3)))

    for q, offset in enumerate(torus.experts()):
        message(q, offset, -1).wait_recv()
    score_out[...] = score_in[...]
    for q, offset in enumerate(torus.experts()):
        message(q, offset, 1).wait_send()
    for t in range(tiles):
        cross(t).wait_send()
    for s in range(NS):
        order = BACK[s // 2]
        for phase in (0, 1):
            for k in range(n[order[phase]] - 1):
                for h in range(2):
                    ring(s, phase, k, h).wait_send()
        for by in range(1, n[order[2]]):
            last(s, by).wait_send()


def back_all(torus, every, gates, wg, wu, wd):
    n = torus.n
    depth = wg.shape[0]
    width = depth // (torus.nzl * n["x"])
    wide = n["x"] * width
    experts = torus.nzh * n["y"] * 2
    bufs = []
    for order in BACK:
        for phase, axis in enumerate(order):
            free = order[phase + 1:]
            shape = (2, n[axis] - 1)
            if "z" in free:
                shape += (torus.nzl, torus.nzh)
            if "y" in free:
                shape += (n["y"],)
            shape += (OCT, wide if "x" in free else width)
            bufs.append(pltpu.VMEM(shape, BF16))
    most = max(n.values()) - 1
    others = len(torus.experts())
    total = experts * NS * OCT
    dma = pltpu.SemaphoreType.DMA
    vm = pltpu.VMEM
    half = (torus.nzl, torus.nzh, n["y"], NS, OCT, wide)
    any_ = pl.BlockSpec(memory_space=pl.ANY)
    vspec = pl.BlockSpec(memory_space=pltpu.VMEM)
    return pl.pallas_call(
        functools.partial(back_kernel, torus, depth, min(512, depth // 2)),
        out_shape=[jax.ShapeDtypeStruct((NS, OCT, width), BF16),
                   jax.ShapeDtypeStruct((experts, OCT, LANE), F32),
                   jax.ShapeDtypeStruct((depth, LANE), BF16),
                   jax.ShapeDtypeStruct((depth, LANE), BF16),
                   jax.ShapeDtypeStruct((LANE, depth), BF16)],
        in_specs=[any_, vspec, any_, any_, any_],
        out_specs=[vspec, vspec, any_, any_, any_],
        scratch_shapes=[vm((2,) + half, BF16), vm(half, BF16), vm((depth, 2 * LANE), BF16), vm((LANE, depth), BF16),
                        vm((2 * LANE, total), BF16), vm((LANE, total), BF16), vm((torus.nzh, OCT, LANE), F32),
                        vm((experts, OCT, LANE), F32), *bufs, dma((3,)), dma((NS,)), dma((NS,)),
                        dma((NS, 2, most, 2)), dma((NS, 2, most, 2)), dma((NS, most)), dma((NS, most)),
                        dma((others,)), dma((others,))],
        compiler_params=pltpu.CompilerParams(
            collective_id=1, has_side_effects=True, vmem_limit_bytes=67043328),
        name="back_all",
    )(every, gates, wg, wu, wd)


def on_device(torus, tokens, grad_out, gates, expert_ids, gate_weight, up_weight, down_weight):
    count, depth = tokens.shape
    n = torus.n
    n_et = torus.nzl * n["x"]
    n_exp = torus.nzh * n["y"] * 2
    share = depth // (2 * n["x"])
    experts = jnp.arange(LANE, dtype=jnp.int32)
    chosen = expert_ids[:, :, None] == experts[None, None, :]
    table = jnp.sum(jnp.where(chosen, gates[:, :, None].astype(F32), 0.0), axis=1).astype(BF16)
    packed = jnp.stack([tokens, grad_out], axis=1).reshape(count, 2, 2, n["x"], share)
    packed = packed.transpose(0, 1, 3, 2, 4).reshape(count, n_et, 2 * share)
    packed = jnp.concatenate([packed, jnp.broadcast_to(table[:, None], (count, n_et, LANE))], axis=2)
    blk = lax.all_to_all(packed.reshape(count, n_et * (2 * share + LANE)), "et", split_axis=1, concat_axis=0, tiled=True)
    rows = n_et * count
    sel = blk[:, 2 * share:].astype(F32).T[:n_exp]
    sel = jnp.pad(sel, ((0, 0), (0, LANE - rows)))[:, None, :]
    blk = blk[:, :2 * share].reshape(NS // 2, ROWS, 2, share).transpose(2, 0, 1, 3)
    every, scale = gather_all(torus, blk, sel)
    scale = scale[:, 0, :rows].reshape(2, n_exp // 2, NS // 2, ROWS).transpose(2, 0, 1, 3)
    scale = jnp.broadcast_to(scale.reshape(NS, n_exp // 2 * ROWS, 1), (NS, n_exp // 2 * ROWS, LANE))
    mine, score, dg, du, dd = back_all(torus, every, scale, gate_weight[0], up_weight[0], down_weight[0])
    me = lax.axis_index("exp")
    per = 2 * n["y"]
    score = score[:, :NS // 2, :per * ROWS].reshape(n_exp, NS // 2, per, ROWS)
    score = lax.dynamic_index_in_dim(score, lax.rem(me, per), axis=2, keepdims=False)
    score = jnp.pad(score.reshape(n_exp, rows).T.astype(BF16), ((0, 0), (0, LANE - n_exp)))
    mine = jnp.concatenate([mine.reshape(rows, mine.shape[2]), score], axis=1)
    owned = lax.all_to_all(mine, "et", split_axis=0, concat_axis=1, tiled=True)
    cols = depth // n_et
    owned = owned.reshape(count, n_et, cols + LANE)
    input_grad = owned[:, :, :cols].reshape(count, depth)
    scores = jnp.sum(owned[:, :, cols:].astype(F32), axis=1)
    gate_grad = jnp.sum(jnp.where(chosen, scores[:, None, :], 0.0), axis=2)
    return input_grad, gate_grad, dg[None], du[None], dd[None]


def solution(mesh, dims=(4, 4, 4, 2)):
    placed = (
        P(("exp", "et"), None),
        P(("exp", "et"), None),
        P(("exp", "et"), None),
        P(("exp", "et"), None),
        P("exp", None, "et"),
        P("exp", None, "et"),
        P("exp", "et", None),
    )
    return jax.shard_map(
        functools.partial(on_device, Torus(*dims)),
        mesh=mesh,
        in_specs=placed,
        out_specs=(
            P(("exp", "et"), None),
            P(("exp", "et"), None),
            P("exp", None, "et"),
            P("exp", None, "et"),
            P("exp", "et", None),
        ),
        check_vma=False,
    )
```

time: 419 us -> 275 us (0.66)
  Pallas kernels: 0 us -> 232 us
  waiting for transfers between devices: 200 us -> 11 us
  blocking collectives: 95.2 us -> 0 us
  matrix products: 50.5 us -> 0 us
  local copies, waits for them, and re-layouts: 30.8 us -> 15.1 us
  between operations: 15.2 us -> 0.79 us
  starting transfers between devices: 23.9 us -> 11.1 us
    pallas_call x0 -> x2, Pallas kernels: none -> 232 us  [the longest x1 123 us: gather_all(): pl.pallas_call(functools.partial(gather_kernel, torus, width), out_shape=...]
    all_gather x2 -> x0, waiting for transfers between devices: 112 us -> none  [the longest x1 76.6 us: on_device(): lax.all_gather(rows_dy, 'et', axis=0, tiled=True)]
    all_to_all x2 -> x0, blocking collectives: 77.7 us -> none  [the longest x1 42.3 us: on_device(): lax.all_to_all(buf_dy, 'exp', split_axis=0, concat_axis=0, tiled=True)]
    reduce_scatter x1 -> x0, waiting for transfers between devices: 73.1 us -> none  [on_device(): lax.psum_scatter(folded[3].astype(jnp.bfloat16), 'et', scatter_dimension=...]
    dot_general x8 -> x0, matrix products: 50.5 us -> none  [the longest x1 10.3 us: expert_terms(): lax.dot_general(grad_up, w_up, (((1,), (1,)), ((), ())), preferred_elemen...]
    unnamed x1 -> x0, blocking collectives: 17.5 us -> none
    all_to_all x3 -> x2, starting transfers between devices: 23.6 us -> 11.1 us  [the longest x1 5.76 us: on_device(): lax.all_to_all(packed.reshape(count, n_et * (2 * share + LANE)), 'et', sp...]
    scatter x3 -> x0, local copies, waits for them, and re-layouts: 6.23 us -> none  [pack_rows(): jnp.zeros((total,) + values.shape[1:], values.dtype).at[slots].set(values)]
  transfers between devices with their start and end apart: 6 -> 2, of which waited for: 5 -> 2; matrix products, arithmetic and copies ran while one was open for 10% -> 0% of each run, Pallas kernels for 0% -> 0%
where the time goes in v2:
time: 275 us; the launch traced here: 274 us
  Pallas kernels  232 us (84%)
  local copies, waits for them, and re-layouts  15.1 us (5%)
  starting transfers between devices  11.1 us (4%)
  waiting for transfers between devices  11 us (4%)
  other arithmetic  4.44 us (2%)
    pallas_call x1, Pallas kernels, gather_all(): pl.pallas_call(functools.partial(gather_kernel, torus, width), out_shape=...  123 us
    pallas_call x1, Pallas kernels, back_all(): pl.pallas_call(functools.partial(back_kernel, torus, depth, min(512, dept...  109 us
    unnamed x8, local copies, waits for them, and re-layouts  6.49 us
    all_to_all x1, starting transfers between devices, on_device(): lax.all_to_all(packed.reshape(count, n_et * (2 * share + LANE)), 'et', sp...  5.76 us
    all_to_all x1, waiting for transfers between devices, on_device(): lax.all_to_all(packed.reshape(count, n_et * (2 * share + LANE)), 'et', sp...  5.74 us
  transfers between devices with their start and end apart: 2, of which 2 were waited for; matrix products, arithmetic and copies ran while one was open for 0% of the time, Pallas kernels for 0%

profile of v2, /device:TPU:32, one launch (start us, length us, event | category | flops | bytes accessed | tf_op | source)
XLA Modules:
  0.0 274.2 jit_solution(18439595859110672382)
XLA Ops:
  0.6 0.7 convert_element_type.28
  1.3 1.0 stack.10
  2.4 1.0 stack.9
  3.8 0.8 fusion.1
  4.6 0.7 copy.39
  5.3 5.8 %all-to-all-start = ((bf16[6,8,1920]{2,0,1:T(8,128)(2,1)}), bf16[6,8,1920]{2,0,1:T(8,128)(2,1)S(1)}, u32[]{:S(2)}, u32[]{:S(2)}) async-start(bf16[6,8,1920]{2,0,1:T(8,128)(2,1)} %copy.39), calls=%async_computation | async-start | bytes 491520 | tf_op jit(solution)/shard_map/all_to_all | solution.py:610
  11.0 5.7 %all-to-all-done = bf16[6,8,1920]{2,0,1:T(8,128)(2,1)S(1)} async-done(((bf16[6,8,1920]{2,0,1:T(8,128)(2,1)}), bf16[6,8,1920]{2,0,1:T(8,128)(2,1)S(1)}, u32[]{:S(2)}, u32[]{:S(2)}) %all-to-all-start) | async-done | bytes 184352 | tf_op jit(solution)/shard_map/all_to_all | solution.py:610
  16.9 0.7 copy.47
  17.8 0.6 pad_convert_fusion
  18.4 123.1 %gather_all.1 = (bf16[2,2,4,4,2,3,16,3584]{7,6,5,4,3,2,1,0:T(8,128)(2,1)}, f32[32,1,128]{2,1,0:T(1,128)}) custom-call(bf16[2,3,16,896]{3,2,1,0:T(8,128)(2,1)} %bitcast.33, f32[32,1,128]{2,1,0:T(1,128)} %bitcast.39), custom_call_target="tpu_custom_call" | custom-call | tf_op jit(solution)/shard_map/gather_all/pallas_call | solution.py:230
  141.5 0.8 copy.42
  142.6 1.1 broadcast_in_dim.59.gates
  143.7 108.7 %back_all.1 = (bf16[6,8,896]{2,1,0:T(8,128)(2,1)}, f32[32,8,128]{2,1,0:T(8,128)}, bf16[7168,128]{1,0:T(8,128)(2,1)}, bf16[7168,128]{1,0:T(8,128)(2,1)}, bf16[128,7168]{1,0:T(8,128)(2,1)}) custom-call(bf16[2,2,4,4,2,3,16,3584]{7,6,5,4,3,2,1,0:T(8,128)(2,1)} %get-tuple-element.12.every, f32[6,256,128]{2,1,0:T(8,128)} %broadcast_in_dim.59.gates, ...), custom_call_target="tpu_custom_call" | custom-call | tf_op jit(solution)/shard_map/back_all/pallas_call | solution.py:578
  252.4 0.9 slice.26
  253.5 0.9 concatenate.13
  254.5 0.7 pad_maximum_fusion.1
  255.1 5.3 %all-to-all-start.1 = ((bf16[8,6,1024]{2,1,0:T(8,128)(2,1)}), bf16[8,6,1024]{2,1,0:T(8,128)(2,1)S(1)}, u32[]{:S(2)}, u32[]{:S(2)}) async-start(bf16[8,6,1024]{2,1,0:T(8,128)(2,1)} %pad_maximum_fusion.1), calls=%async_computation.1 | async-start | bytes 262144 | tf_op jit(solution)/shard_map/all_to_all | solution.py:625
  260.4 5.3 %all-to-all-done.1 = bf16[8,6,1024]{2,1,0:T(8,128)(2,1)S(1)} async-done(((bf16[8,6,1024]{2,1,0:T(8,128)(2,1)}), bf16[8,6,1024]{2,1,0:T(8,128)(2,1)S(1)}, u32[]{:S(2)}, u32[]{:S(2)}) %all-to-all-start.1) | async-done | bytes 98336 | tf_op jit(solution)/shard_map/all_to_all | solution.py:625
  265.7 0.7 slice.32
  266.4 1.4 select_reduce_fusion
  267.8 3.0 %copy.51 = bf16[1,7168,128]{2,1,0:T(8,128)(2,1)} copy(bf16[1,7168,128]{2,1,0:T(8,128)(2,1)} %bitcast.28) | data formatting | bytes 3670016
  270.8 1.2 copy.52
  272.0 0.9 copy-done
  272.9 1.2 copy.53
  (22 shorter events, 1.2 us)
Async XLA Ops:
  5.3 11.5 %all-to-all-start = ((bf16[6,8,1920]{2,0,1:T(8,128)(2,1)}), bf16[6,8,1920]{2,0,1:T(8,128)(2,1)S(1)}, u32[]{:S(2)}, u32[]{:S(2)}) async-start(bf16[6,8,1920]{2,0,1:T(8,128)(2,1)} %copy.39), calls=%async_computation | async-start | bytes 491520 | tf_op jit(solution)/shard_map/all_to_all | solution.py:610
  255.1 10.5 %all-to-all-start.1 = ((bf16[8,6,1024]{2,1,0:T(8,128)(2,1)}), bf16[8,6,1024]{2,1,0:T(8,128)(2,1)S(1)}, u32[]{:S(2)}, u32[]{:S(2)}) async-start(bf16[8,6,1024]{2,1,0:T(8,128)(2,1)} %pad_maximum_fusion.1), calls=%async_computation.1 | async-start | bytes 262144 | tf_op jit(solution)/shard_map/all_to_all | solution.py:625
  267.8 3.0 %copy-start.1 = (bf16[7168,128]{1,0:T(8,128)(2,1)S(1)}, bf16[7168,128]{1,0:T(8,128)(2,1)}, u32[]{:S(2)}) copy-start(bf16[7168,128]{1,0:T(8,128)(2,1)} %get-tuple-element.17) | copy-start | bytes 5505028
  270.8 2.2 copy-start

commit v3 on v2

--- a/solution.py
+++ b/solution.py
@@ -61,6 +61,16 @@
         out = self.moved(pos, "y", sign * y)
         out["z"] = self.shift(pos, "z", sign * h * self.nzl)
         return out, (1 - core if c else core)
+
+    def peers(self):
+        return [(l, x) for l in range(self.nzl) for x in range(self.n["x"]) if l or x]
+
+    def peer(self, pos, core, offset, sign):
+        l, x = offset
+        out = self.moved(pos, "x", sign * x)
+        zl, zh = self.split(pos["z"])
+        out["z"] = zh * self.nzl + (lax.rem(zl + l, self.nzl) if l else zl)
+        return self.device(out, core)
 
     def greet(self, pos, core):
         seen, partners = set(), []
@@ -75,6 +85,9 @@
             for by in range(1, self.n[axis]):
                 if (axis, by) not in seen:
                     partners.append(self.device(self.moved(pos, axis, by), core))
+        for l, x in self.peers():
+            if l and x:
+                partners.append(self.peer(pos, core, (l, x), 1))
         barrier = pltpu.get_barrier_semaphore()
         for p in partners:
             pl.semaphore_signal(barrier, inc=1, device_id=p, device_id_type=MESH)
@@ -114,12 +127,40 @@
     return w
 
 
-def gather_kernel(torus, width, blk, sel, out, gate_out, gate_in, loc, p1_send, p1_recv, send, recv, sib_send,
-                  sib_recv, g_send, g_recv):
+def gather_kernel(torus, width, packed, sel, out, gate_out, gate_in, gate_all, inbox, stack, blk, loc, p1_send, p1_recv,
+                  send, recv, sib_send, sib_recv, g_send, g_recv, e_send, e_recv, h_send, h_recv):
     pos, core = torus.here()
     me = torus.device(pos, core)["exp"]
+    my_et = torus.device(pos, core)["et"]
     sibling = torus.device(pos, 1 - core)
     torus.greet(pos, core)
+
+    def hand(q, offset, sign):
+        to = torus.peer(pos, core, offset, sign)
+        slot = my_et if sign > 0 else to["et"]
+        return remote(packed.at[to["et"]], inbox.at[slot], e_send.at[q], e_recv.at[q], to)
+
+    def share(q, offset, sign):
+        to = torus.peer(pos, core, offset, sign)
+        slot = my_et if sign > 0 else to["et"]
+        return remote(gate_in, gate_all.at[slot], h_send.at[q], h_recv.at[q], to)
+
+    for q, offset in enumerate(torus.peers()):
+        hand(q, offset, 1).start()
+    for q, offset in enumerate(torus.experts()):
+        p, k = torus.other_expert(pos, core, offset, 1)
+        to = torus.device(p, k)
+        remote(sel.at[to["exp"]], gate_in.at[me], g_send.at[q], g_recv.at[q], to).start()
+    gate_in[me] = sel[me]
+    inbox[my_et] = packed[my_et]
+    for q, offset in enumerate(torus.peers()):
+        hand(q, offset, -1).wait_recv()
+    count = packed.shape[1]
+    for i in range(packed.shape[0]):
+        stack[i * count:(i + 1) * count, :] = inbox[i].astype(F32)
+    for d in range(2):
+        for o in range(NS // 2):
+            blk[d, o] = stack[o * ROWS:(o + 1) * ROWS, d * width:(d + 1) * width].astype(BF16)
 
     def region(s, phase, shift, part=None, c=core):
         order = ORDERS[s // 2]
@@ -131,14 +172,26 @@
         zl, zh, y, col = chosen_part(torus, at, part, width)
         return out.at[zl, s % 2, zh, y, c, s // 2, :, col]
 
-    def first(s, by):
-        axis = ORDERS[s // 2][0]
-        return remote(blk.at[s % 2, s // 2], region(s, 0, 0), p1_send.at[s, by - 1], p1_recv.at[s, by - 1],
-                      torus.device(torus.moved(pos, axis, by), core))
-
-    def first_landed(s, by):
-        here = region(s, 0, -by)
-        return remote(here, here, p1_send.at[s, by - 1], p1_recv.at[s, by - 1], sibling)
+    def reach(s):
+        n = torus.n[ORDERS[s // 2][0]]
+        up = n // 2 if s % 2 == 0 else n - 1 - n // 2
+        return up, n - 1 - up
+
+    def first(s, d, hop):
+        i = hop - 1 if d > 0 else reach(s)[0] + hop - 1
+        here = region(s, 0, -d * (hop - 1))
+        src = blk.at[s % 2, s // 2] if hop == 1 else here
+        return remote(src, here, p1_send.at[s, i], p1_recv.at[s, i],
+                      torus.device(torus.moved(pos, ORDERS[s // 2][0], d), core))
+
+    def first_landed(s, d, hop):
+        i = hop - 1 if d > 0 else reach(s)[0] + hop - 1
+        here = region(s, 0, -d * hop)
+        return remote(here, here, p1_send.at[s, i], p1_recv.at[s, i], sibling)
+
+    def chain(s):
+        up, down = reach(s)
+        return [(d, h) for h in range(1, max(up, down) + 1) for d in (1, -1) if h <= (up if d > 0 else down)]
 
     def ring(s, phase, k, part):
         d = 1 if s % 2 == 0 else -1
@@ -159,22 +212,31 @@
         return pltpu.make_async_copy(blk.at[s % 2, s // 2], region(s, 0, 0), loc.at[s])
 
     for s in range(NS):
-        for by in range(1, torus.n[ORDERS[s // 2][0]]):
-            first(s, by).start()
+        for d, h in chain(s):
+            if h == 1:
+                first(s, d, 1).start()
         own(s).start()
-    for q, offset in enumerate(torus.experts()):
-        p, k = torus.other_expert(pos, core, offset, 1)
-        to = torus.device(p, k)
-        remote(sel.at[to["exp"]], gate_in.at[me], g_send.at[q], g_recv.at[q], to).start()
-    gate_in[me] = sel[me]
     for s in range(NS):
         own(s).wait()
-        for by in range(1, torus.n[ORDERS[s // 2][0]]):
-            first_landed(s, by).wait_recv()
-        for part in range(2):
-            ring(s, 1, 0, part).start()
-        whole = region(s, 1, 0)
-        across(s, whole, whole).start()
+    for hop in range(1, max(torus.n.values()) // 2 + 1):
+        for s in range(NS):
+            mine = [(d, h) for d, h in chain(s) if h == hop]
+            for d, h in mine:
+                first_landed(s, d, h).wait_recv()
+                if (d, h + 1) in chain(s):
+                    first(s, d, h + 1).start()
+            if mine and hop == max(h for _, h in chain(s)):
+                for part in range(2):
+                    ring(s, 1, 0, part).start()
+                whole = region(s, 1, 0)
+                across(s, whole, whole).start()
+    for q, offset in enumerate(torus.experts()):
+        p, k = torus.other_expert(pos, core, offset, -1)
+        came = torus.device(p, k)
+        remote(sel.at[me], gate_in.at[came["exp"]], g_send.at[q], g_recv.at[q], came).wait_recv()
+    for q, offset in enumerate(torus.peers()):
+        share(q, offset, 1).start()
+    gate_all[my_et] = gate_in[...]
     events = []
     for s in range(NS):
         order = ORDERS[s // 2]
@@ -198,15 +260,16 @@
         d = 1 if s % 2 == 0 else -1
         here = region(s, phase, -d * (k + 1), part)
         across(s, here, here).start()
-    for q, offset in enumerate(torus.experts()):
-        p, k = torus.other_expert(pos, core, offset, -1)
-        came = torus.device(p, k)
-        remote(sel.at[me], gate_in.at[came["exp"]], g_send.at[q], g_recv.at[q], came).wait_recv()
-    gate_out[...] = gate_in[...]
+    for q, offset in enumerate(torus.peers()):
+        share(q, offset, -1).wait_recv()
+    gate_out[...] = gate_all[...]
+    for q, offset in enumerate(torus.peers()):
+        share(q, offset, 1).wait_send()
+        hand(q, offset, 1).wait_send()
     for s in range(NS):
         order = ORDERS[s // 2]
-        for by in range(1, torus.n[order[0]]):
-            first(s, by).wait_send()
+        for d, h in chain(s):
+            first(s, d, h).wait_send()
         for phase in (1, 2):
             for k in range(torus.n[order[phase]] - 1):
                 for part in range(2):
@@ -220,38 +283,43 @@
         remote(sel.at[to["exp"]], gate_in.at[me], g_send.at[q], g_recv.at[q], to).wait_send()
 
 
-def gather_all(torus, blk, sel):
-    width = blk.shape[3]
+def gather_all(torus, packed, sel):
+    width = packed.shape[2] // 2
     n = torus.n
     shape = (torus.nzl, 2, torus.nzh, n["y"], 2, NS // 2, ROWS, n["x"] * width)
     most = max(n.values()) - 1
-    others = len(torus.experts())
+    others, peers = len(torus.experts()), len(torus.peers())
+    gates = (packed.shape[0],) + sel.shape
     dma = pltpu.SemaphoreType.DMA
+    vm = pltpu.VMEM
     return pl.pallas_call(
         functools.partial(gather_kernel, torus, width),
-        out_shape=[jax.ShapeDtypeStruct(shape, blk.dtype), jax.ShapeDtypeStruct(sel.shape, sel.dtype)],
+        out_shape=[jax.ShapeDtypeStruct(shape, packed.dtype), jax.ShapeDtypeStruct(gates, sel.dtype)],
         in_specs=[pl.BlockSpec(memory_space=pltpu.VMEM)] * 2,
         out_specs=[pl.BlockSpec(memory_space=pl.ANY), pl.BlockSpec(memory_space=pltpu.VMEM)],
-        scratch_shapes=[pltpu.VMEM(sel.shape, sel.dtype), dma((NS,)), dma((NS, most)), dma((NS, most)),
+        scratch_shapes=[vm(sel.shape, sel.dtype), vm(gates, sel.dtype), vm(packed.shape, packed.dtype),
+                        vm((NS * OCT, 2 * width), F32), vm((2, NS // 2, ROWS, width), packed.dtype),
+                        dma((NS,)), dma((NS, most)), dma((NS, most)),
                         dma((NS, 2, most, 2)), dma((NS, 2, most, 2)), dma((NS,)), dma((NS,)),
-                        dma((others,)), dma((others,))],
+                        dma((others,)), dma((others,)), dma((peers,)), dma((peers,)), dma((peers,)), dma((peers,))],
         compiler_params=pltpu.CompilerParams(collective_id=0, has_side_effects=True),
         name="gather_all",
-    )(blk, sel)
+    )(packed, sel)
 
 
 BACK = tuple(tuple(reversed(o)) for o in ORDERS)
 
 
 def back_kernel(torus, depth, tile_cols, every, gates, wg, wu, wd, out, score_out, dg, du, dd,
-                part, theirs, wcat, wdown, gt, wt, score, score_in, b0, b1, b2, b3, b4, b5, b6, b7, b8,
-                w_sem, sib_send, sib_recv, send, recv, p3_send, p3_recv, s_send, s_recv):
+                part, theirs, wcat, wdown, gt, wt, score, score_in, score_all, fin, ship, inbox, b0, b1, b2, b3, b4, b5, b6, b7, b8,
+                w_sem, sib_send, sib_recv, send, recv, p3_send, p3_recv, s_send, s_recv, e_send, e_recv, h_send, h_recv):
     bufs = (b0, b1, b2, b3, b4, b5, b6, b7, b8)
     n = torus.n
     width = depth // (torus.nzl * n["x"])
     wide = n["x"] * width
     pos, core = torus.here()
     me = torus.device(pos, core)["exp"]
+    my_et = torus.device(pos, core)["et"]
     sibling = torus.device(pos, 1 - core)
     hz = torus.nzh // 2
     group = hz * n["y"] * 2
@@ -346,9 +414,7 @@
                 y = iy + ybase
             else:
                 y = y0
-            g = got[where + (slice(None), slice(None))].astype(F32)
-            p = part[core, zl, zh, y, s, :, col0].astype(F32)
-            part[core, zl, zh, y, s, :, col0] = (p + g).astype(BF16)
+            part[core, zl, zh, y, s, :, col0] += got[where + (slice(None), slice(None))]
             return carry
 
         lax.fori_loop(0, nzl * nzh * ny, one, 0)
@@ -411,9 +477,8 @@
             gt[LANE:, cols] = grad_up.T.astype(BF16)
             wt[:, cols] = (scale * act).T.astype(BF16)
             sums = jnp.sum((act * back).T, axis=0, keepdims=True)
-            each = rows // hz
-            for z in range(hz):
-                score[hh * hz + z, o:o + 1, :each] = sums[:, z * each:(z + 1) * each]
+            for g in range(group):
+                score[hh * group + g, :, o * ROWS:(o + 1) * ROWS] = sums[:, g * ROWS:(g + 1) * ROWS]
             both = jnp.concatenate([grad_gate.astype(BF16), grad_up.astype(BF16)], axis=1)
             for j in range(torus.nzl * n["x"]):
                 zl, x = j // n["x"], j % n["x"]
@@ -433,13 +498,22 @@
     def message(q, offset, sign):
         p, k = torus.other_expert(pos, core, offset, sign)
         other = torus.device(p, k)
-        zh = torus.split(p["z"])[1]
-        mine = score.at[zh] if sign > 0 else score.at[0]
-        return remote(mine, score_in.at[me if sign > 0 else other["exp"]], s_send.at[q], s_recv.at[q], other)
+        return remote(score.at[other["exp"]], score_in.at[me if sign > 0 else other["exp"]],
+                      s_send.at[q], s_recv.at[q], other)
+
+    def share(q, offset, sign):
+        to = torus.peer(pos, core, offset, sign)
+        slot = my_et if sign > 0 else to["et"]
+        return remote(score_in, score_all.at[slot], h_send.at[q], h_recv.at[q], to)
+
+    def hand(q, offset, sign):
+        to = torus.peer(pos, core, offset, sign)
+        slot = my_et if sign > 0 else to["et"]
+        return remote(ship.at[to["et"]], inbox.at[slot], e_send.at[q], e_recv.at[q], to)
 
     for q, offset in enumerate(torus.experts()):
         message(q, offset, 1).start()
-    score_in[me] = score[torus.split(pos["z"])[1]]
+    score_in[me] = score[me]
 
     def exchange(xt, dt, sg, su, sd, x_sem, d_sem, o_sem):
         units = depth // tile_cols
@@ -496,6 +570,12 @@
         events.sort()
         done = 0
         for i, (_, s, phase, k, h) in enumerate(events):
+            if i == 4:
+                for q, offset in enumerate(torus.experts()):
+                    message(q, offset, -1).wait_recv()
+                for q, offset in enumerate(torus.peers()):
+                    share(q, offset, 1).start()
+                score_all[my_et] = score_in[...]
             while done < units and done * len(events) * 3 // 5 <= i * units:
                 unit(done)
                 done += 1
@@ -519,7 +599,13 @@
                 for by in range(1, n[order[2]]):
                     last(s, by).wait_recv()
                     total = total + bufs[s // 2 * 3 + 2][s % 2, by - 1].astype(F32)
-                out[s] = total.astype(BF16)
+                fin[s * OCT:(s + 1) * OCT, :] = total
+        count = out.shape[1]
+        for i in range(out.shape[0]):
+            ship[i] = fin[i * count:(i + 1) * count, :].astype(BF16)
+        for q, offset in enumerate(torus.peers()):
+            hand(q, offset, 1).start()
+        inbox[my_et] = ship[my_et]
         while done < units:
             unit(done)
             done += 1
@@ -533,9 +619,14 @@
     pl.run_scoped(exchange, tiled, tiled, stage, stage, pltpu.VMEM((2, LANE, tile_cols), BF16),
                   dma((2, tiles)), dma((2, tiles)), dma((2, 3)))
 
-    for q, offset in enumerate(torus.experts()):
-        message(q, offset, -1).wait_recv()
-    score_out[...] = score_in[...]
+    for q, offset in enumerate(torus.peers()):
+        hand(q, offset, -1).wait_recv()
+        share(q, offset, -1).wait_recv()
+    out[...] = inbox[...]
+    score_out[...] = score_all[...]
+    for q, offset in enumerate(torus.peers()):
+        hand(q, offset, 1).wait_send()
+        share(q, offset, 1).wait_send()
     for q, offset in enumerate(torus.experts()):
         message(q, offset, 1).wait_send()
     for t in range(tiles):
@@ -568,8 +659,10 @@
             shape += (OCT, wide if "x" in free else width)
             bufs.append(pltpu.VMEM(shape, BF16))
     most = max(n.values()) - 1
-    others = len(torus.experts())
+    others, peers = len(torus.experts()), len(torus.peers())
+    n_et = peers + 1
     total = experts * NS * OCT
+    owned = (n_et, NS * OCT // n_et, width)
     dma = pltpu.SemaphoreType.DMA
     vm = pltpu.VMEM
     half = (torus.nzl, torus.nzh, n["y"], NS, OCT, wide)
@@ -577,18 +670,19 @@
     vspec = pl.BlockSpec(memory_space=pltpu.VMEM)
     return pl.pallas_call(
         functools.partial(back_kernel, torus, depth, min(512, depth // 2)),
-        out_shape=[jax.ShapeDtypeStruct((NS, OCT, width), BF16),
-                   jax.ShapeDtypeStruct((experts, OCT, LANE), F32),
+        out_shape=[jax.ShapeDtypeStruct(owned, BF16),
+                   jax.ShapeDtypeStruct((n_et, experts, 1, LANE), F32),
                    jax.ShapeDtypeStruct((depth, LANE), BF16),
                    jax.ShapeDtypeStruct((depth, LANE), BF16),
                    jax.ShapeDtypeStruct((LANE, depth), BF16)],
         in_specs=[any_, vspec, any_, any_, any_],
         out_specs=[vspec, vspec, any_, any_, any_],
         scratch_shapes=[vm((2,) + half, BF16), vm(half, BF16), vm((depth, 2 * LANE), BF16), vm((LANE, depth), BF16),
-                        vm((2 * LANE, total), BF16), vm((LANE, total), BF16), vm((torus.nzh, OCT, LANE), F32),
-                        vm((experts, OCT, LANE), F32), *bufs, dma((3,)), dma((NS,)), dma((NS,)),
+                        vm((2 * LANE, total), BF16), vm((LANE, total), BF16), vm((experts, 1, LANE), F32),
+                        vm((experts, 1, LANE), F32), vm((n_et, experts, 1, LANE), F32), vm((NS * OCT, width), F32),
+                        vm(owned, BF16), vm(owned, BF16), *bufs, dma((3,)), dma((NS,)), dma((NS,)),
                         dma((NS, 2, most, 2)), dma((NS, 2, most, 2)), dma((NS, most)), dma((NS, most)),
-                        dma((others,)), dma((others,))],
+                        dma((others,)), dma((others,)), dma((peers,)), dma((peers,)), dma((peers,)), dma((peers,))],
         compiler_params=pltpu.CompilerParams(
             collective_id=1, has_side_effects=True, vmem_limit_bytes=67043328),
         name="back_all",
@@ -604,30 +698,20 @@
     experts = jnp.arange(LANE, dtype=jnp.int32)
     chosen = expert_ids[:, :, None] == experts[None, None, :]
     table = jnp.sum(jnp.where(chosen, gates[:, :, None].astype(F32), 0.0), axis=1).astype(BF16)
-    packed = jnp.stack([tokens, grad_out], axis=1).reshape(count, 2, 2, n["x"], share)
-    packed = packed.transpose(0, 1, 3, 2, 4).reshape(count, n_et, 2 * share)
-    packed = jnp.concatenate([packed, jnp.broadcast_to(table[:, None], (count, n_et, LANE))], axis=2)
-    blk = lax.all_to_all(packed.reshape(count, n_et * (2 * share + LANE)), "et", split_axis=1, concat_axis=0, tiled=True)
+    both = jnp.stack([tokens, grad_out], axis=0).reshape(2, count, 2, n["x"], share)
+    packed = both.transpose(0, 3, 1, 2, 4).reshape(n_et, count, 2 * share)
+    sel = jnp.pad(table.astype(F32).T[:n_exp], ((0, 0), (0, LANE - count)))[:, None, :]
+    every, scale = gather_all(torus, packed, sel)
     rows = n_et * count
-    sel = blk[:, 2 * share:].astype(F32).T[:n_exp]
-    sel = jnp.pad(sel, ((0, 0), (0, LANE - rows)))[:, None, :]
-    blk = blk[:, :2 * share].reshape(NS // 2, ROWS, 2, share).transpose(2, 0, 1, 3)
-    every, scale = gather_all(torus, blk, sel)
-    scale = scale[:, 0, :rows].reshape(2, n_exp // 2, NS // 2, ROWS).transpose(2, 0, 1, 3)
+    scale = scale[:, :, 0, :count].transpose(1, 0, 2).reshape(2, n_exp // 2, NS // 2, ROWS).transpose(2, 0, 1, 3)
     scale = jnp.broadcast_to(scale.reshape(NS, n_exp // 2 * ROWS, 1), (NS, n_exp // 2 * ROWS, LANE))
-    mine, score, dg, du, dd = back_all(torus, every, scale, gate_weight[0], up_weight[0], down_weight[0])
-    me = lax.axis_index("exp")
-    per = 2 * n["y"]
-    score = score[:, :NS // 2, :per * ROWS].reshape(n_exp, NS // 2, per, ROWS)
-    score = lax.dynamic_index_in_dim(score, lax.rem(me, per), axis=2, keepdims=False)
-    score = jnp.pad(score.reshape(n_exp, rows).T.astype(BF16), ((0, 0), (0, LANE - n_exp)))
-    mine = jnp.concatenate([mine.reshape(rows, mine.shape[2]), score], axis=1)
-    owned = lax.all_to_all(mine, "et", split_axis=0, concat_axis=1, tiled=True)
-    cols = depth // n_et
-    owned = owned.reshape(count, n_et, cols + LANE)
-    input_grad = owned[:, :, :cols].reshape(count, depth)
-    scores = jnp.sum(owned[:, :, cols:].astype(F32), axis=1)
-    gate_grad = jnp.sum(jnp.where(chosen, scores[:, None, :], 0.0), axis=2)
+    owned, score, dg, du, dd = back_all(torus, every, scale, gate_weight[0], up_weight[0], down_weight[0])
+    input_grad = owned.transpose(1, 0, 2).reshape(count, depth)
+    score = score[:, :, 0, :rows].reshape(n_et, n_exp, n_et, count)
+    score = lax.dynamic_index_in_dim(score, lax.axis_index("et"), axis=2, keepdims=False)
+    score = jnp.sum(score.astype(BF16).astype(F32), axis=0)
+    chosen = chosen[:, :, :n_exp]
+    gate_grad = jnp.sum(jnp.where(chosen, score.T[:, None, :], 0.0), axis=2)
     return input_grad, gate_grad, dg[None], du[None], dd[None]
 
 

time: 275 us -> 253 us (0.920)
  starting transfers between devices: 11.1 us -> 0 us
  waiting for transfers between devices: 11 us -> 0 us
  Pallas kernels: 232 us -> 235 us
    all_to_all x2 -> x0, starting transfers between devices: 11.1 us -> none  [the longest x1 5.76 us: on_device(): lax.all_to_all(packed.reshape(count, n_et * (2 * share + LANE)), 'et', sp...]
    all_to_all x2 -> x0, waiting for transfers between devices: 11 us -> none  [the longest x1 5.74 us: on_device(): lax.all_to_all(packed.reshape(count, n_et * (2 * share + LANE)), 'et', sp...]
    pallas_call x1, Pallas kernels: 109 us -> 114 us  [back_all(): pl.pallas_call(functools.partial(back_kernel, torus, depth, min(512, dept...]
    unnamed x8 -> x12, local copies, waits for them, and re-layouts: 6.49 us -> 7.93 us
  transfers between devices with their start and end apart: 2 -> 0, of which waited for: 2 -> 0; matrix products, arithmetic and copies ran while one was open for 0% -> 0% of each run, Pallas kernels for 0% -> 0%
where the time goes in v3:
time: 253 us
  Pallas kernels  235 us (93%)
  local copies, waits for them, and re-layouts  14.6 us (6%)
    pallas_call x1, Pallas kernels, gather_all(): pl.pallas_call(functools.partial(gather_kernel, torus, width), out_shape=...  121 us
    pallas_call x1, Pallas kernels, back_all(): pl.pallas_call(functools.partial(back_kernel, torus, depth, min(512, dept...  114 us
    unnamed x12, local copies, waits for them, and re-layouts  7.93 us

profile of v3, /device:TPU:32, one launch (start us, length us, event | category | flops | bytes accessed | tf_op | source)
XLA Modules:
  0.0 252.8 jit_solution(13193565269165656957)
XLA Ops:
  0.7 1.0 stack.9
  1.7 1.0 stack.10
  2.8 0.2 maximum_bitcast_fusion
  3.0 0.1 reshape.32
  3.1 0.7 copy.28.packed
  3.8 0.1 select_reduce_fusion.1
  3.9 0.1 copy.27
  4.1 0.6 pad_convert_fusion
  4.7 121.4 %gather_all.1 = (bf16[2,2,4,4,2,3,16,3584]{7,6,5,4,3,2,1,0:T(8,128)(2,1)}, f32[8,32,1,128]{3,2,1,0:T(1,128)}) custom-call(bf16[8,6,1792]{2,1,0:T(8,128)(2,1)} %copy.28.packed, f32[32,1,128]{2,1,0:T(1,128)} %bitcast.36), custom_call_target="tpu_custom_call" | custom-call | tf_op jit(solution)/shard_map/gather_all/pallas_call | solution.py:295
  126.1 1.0 copy.29
  127.1 0.1 reshape.33
  127.2 0.1 copy.30
  127.3 0.1 broadcast_in_dim.53
  127.4 1.1 broadcast_in_dim.54.gates
  128.5 113.7 %back_all.1 = (bf16[8,6,896]{2,1,0:T(8,128)(2,1)}, f32[8,32,1,128]{3,2,1,0:T(1,128)}, bf16[7168,128]{1,0:T(8,128)(2,1)}, bf16[7168,128]{1,0:T(8,128)(2,1)}, bf16[128,7168]{1,0:T(8,128)(2,1)}) custom-call(bf16[2,2,4,4,2,3,16,3584]{7,6,5,4,3,2,1,0:T(8,128)(2,1)} %get-tuple-element.12.every, f32[6,256,128]{2,1,0:T(8,128)} %broadcast_in_dim.54.gates, ...), custom_call_target="tpu_custom_call" | custom-call | tf_op jit(solution)/shard_map/back_all/pallas_call | solution.py:671
  242.3 1.0 slice.16
  243.3 0.1 copy.31
  243.4 0.8 iota_compare_fusion
  244.2 0.7 select_reduce_fusion
  244.9 1.6 copy.36
  246.4 3.0 %copy.37 = bf16[1,7168,128]{2,1,0:T(8,128)(2,1)} copy(bf16[1,7168,128]{2,1,0:T(8,128)(2,1)} %bitcast.28) | data formatting | bytes 3670016
  249.4 1.2 copy.38
  250.6 0.9 copy-done
  251.6 1.2 copy.39
  (12 shorter events, 0.2 us)
Async XLA Ops:
  0.6 3.2 %copy-start.3 = (bf16[6,8]{1,0:T(8,128)(2,1)S(1)}, bf16[6,8]{1,0:T(8,128)(2,1)}, u32[]{:S(2)}) copy-start(bf16[6,8]{1,0:T(8,128)(2,1)} %param.9) | copy-start | bytes 292
  0.6 3.2 %copy-start.2 = (s32[6,8]{1,0:T(8,128)S(1)}, s32[6,8]{1,0:T(8,128)}, u32[]{:S(2)}) copy-start(s32[6,8]{1,0:T(8,128)} %param.10) | copy-start | bytes 580
  246.4 3.0 %copy-start.1 = (bf16[7168,128]{1,0:T(8,128)(2,1)S(1)}, bf16[7168,128]{1,0:T(8,128)(2,1)}, u32[]{:S(2)}) copy-start(bf16[7168,128]{1,0:T(8,128)(2,1)} %get-tuple-element.17) | copy-start | bytes 5505028
  249.4 2.2 copy-start

commit v4 on v3

--- a/solution.py
+++ b/solution.py
@@ -193,17 +193,32 @@
         up, down = reach(s)
         return [(d, h) for h in range(1, max(up, down) + 1) for d in (1, -1) if h <= (up if d > 0 else down)]
 
+    def stretch(s, phase, shift, part):
+        d = 1 if s % 2 == 0 else -1
+        if phase == 1:
+            return region(s, 1, shift, part)
+        order = ORDERS[s // 2]
+        at = dict(pos)
+        at[order[0]] = None
+        at[order[1]] = torus.shift(pos, order[1], -d * part)
+        at[order[2]] = torus.shift(pos, order[2], shift)
+        zl, zh, y, col = chosen_part(torus, at, None, width)
+        return out.at[zl, s % 2, zh, y, core, s // 2, :, col]
+
     def ring(s, phase, k, part):
         d = 1 if s % 2 == 0 else -1
-        here = region(s, phase, -d * k, part)
+        here = stretch(s, phase, -d * k, part)
         i = phase - 1
         return remote(here, here, send.at[s, i, k, part], recv.at[s, i, k, part],
                       torus.device(torus.moved(pos, ORDERS[s // 2][phase], d), core))
 
     def landed(s, phase, k, part):
         d = 1 if s % 2 == 0 else -1
-        here = region(s, phase, -d * (k + 1), part)
+        here = stretch(s, phase, -d * (k + 1), part)
         return remote(here, here, send.at[s, phase - 1, k, part], recv.at[s, phase - 1, k, part], sibling)
+
+    def parts(s, phase):
+        return 2 if phase == 1 else torus.n[ORDERS[s // 2][1]]
 
     def across(s, src, dst):
         return remote(src, dst, sib_send.at[s], sib_recv.at[s], sibling)
@@ -228,6 +243,7 @@
             if mine and hop == max(h for _, h in chain(s)):
                 for part in range(2):
                     ring(s, 1, 0, part).start()
+                ring(s, 2, 0, 0).start()
                 whole = region(s, 1, 0)
                 across(s, whole, whole).start()
     for q, offset in enumerate(torus.experts()):
@@ -240,25 +256,31 @@
     events = []
     for s in range(NS):
         order = ORDERS[s // 2]
-        at = 0.0
-        for phase in (1, 2):
-            w = volume(torus, order[:phase]) * (1.5 if phase == 1 else 1.0)
-            for k in range(torus.n[order[phase]] - 1):
-                for part in range(2):
-                    at += w / 2 + 0.5
-                    events.append((at, s, phase, k, part))
-            at += 1.0
+        base = volume(torus, order[:1]) * 0.7
+        at = ready = 3.0 if order[0] == "x" else 12.0
+        when = [at]
+        for k in range(torus.n[order[1]] - 1):
+            for part in range(2):
+                at += base / 2 * 1.3 + 0.7
+                events.append((at, s, 1, k, part))
+            when.append(at)
+        at = ready
+        for k in range(torus.n[order[2]] - 1):
+            later = []
+            for part in range(torus.n[order[1]]):
+                at = max(at, when[part] + 1.5) + base
+                events.append((at, s, 2, k, part))
+                later.append(at)
+            when = later
     for _, s, phase, k, part in sorted(events):
         order = ORDERS[s // 2]
-        arrived = landed(s, phase, k, part)
-        arrived.wait_recv()
+        landed(s, phase, k, part).wait_recv()
         if k + 1 < torus.n[order[phase]] - 1:
             ring(s, phase, k + 1, part).start()
-        elif phase == 1 and part == 1:
-            for half in range(2):
-                ring(s, 2, 0, half).start()
+        if phase == 1 and part == 1:
+            ring(s, 2, 0, k + 1).start()
         d = 1 if s % 2 == 0 else -1
-        here = region(s, phase, -d * (k + 1), part)
+        here = stretch(s, phase, -d * (k + 1), part)
         across(s, here, here).start()
     for q, offset in enumerate(torus.peers()):
         share(q, offset, -1).wait_recv()
@@ -272,7 +294,7 @@
             first(s, d, h).wait_send()
         for phase in (1, 2):
             for k in range(torus.n[order[phase]] - 1):
-                for part in range(2):
+                for part in range(parts(s, phase)):
                     ring(s, phase, k, part).wait_send()
         whole, other = region(s, 3, 0), region(s, 3, 0, None, 1 - core)
         across(s, whole, whole).wait_send()
@@ -300,7 +322,7 @@
         scratch_shapes=[vm(sel.shape, sel.dtype), vm(gates, sel.dtype), vm(packed.shape, packed.dtype),
                         vm((NS * OCT, 2 * width), F32), vm((2, NS // 2, ROWS, width), packed.dtype),
                         dma((NS,)), dma((NS, most)), dma((NS, most)),
-                        dma((NS, 2, most, 2)), dma((NS, 2, most, 2)), dma((NS,)), dma((NS,)),
+                        dma((NS, 2, most, 4)), dma((NS, 2, most, 4)), dma((NS,)), dma((NS,)),
                         dma((others,)), dma((others,)), dma((peers,)), dma((peers,)), dma((peers,)), dma((peers,))],
         compiler_params=pltpu.CompilerParams(collective_id=0, has_side_effects=True),
         name="gather_all",
@@ -345,25 +367,21 @@
         at[order[phase]] = torus.shift(pos, order[phase], shift)
         return at
 
-    def piece(at, s, h):
-        zl, zh, y, col = chosen_part(torus, at, h, width)
-        return part.at[core, zl, zh, y, s, :, col]
-
-    def slot(s, phase, k, h):
-        ref = bufs[s // 2 * 3 + phase].at[s % 2, k]
-        if h is None:
-            return ref
-        order = BACK[s // 2]
-        if "z" in order[phase + 1:]:
-            return ref.at[h]
-        if "y" in order[phase + 1:]:
-            return ref.at[pl.ds(h * (n["y"] // 2), n["y"] // 2)]
-        return ref.at[:, pl.ds(h * (n["x"] // 2) * width, n["x"] // 2 * width)]
-
-    def ring(s, phase, k, h):
+    def spot(s, phase, shift, q):
+        at = place(s, phase, shift)
+        if phase == 0:
+            d = 1 if s % 2 == 0 else -1
+            at[BACK[s // 2][1]] = torus.shift(pos, BACK[s // 2][1], -d * (q + 1))
+        return at
+
+    def slot(s, phase, k, q):
+        ref = bufs[s // 2 * 3 + phase]
+        return ref.at[s % 2, k, q] if phase == 0 else ref.at[s % 2, k]
+
+    def ring(s, phase, k, q):
         d = 1 if s % 2 == 0 else -1
-        return remote(piece(place(s, phase, -d * (k + 1)), s, h), slot(s, phase, k, h),
-                      send.at[s, phase, k, h], recv.at[s, phase, k, h],
+        return remote(block(spot(s, phase, -d * (k + 1), q), s), slot(s, phase, k, q),
+                      send.at[s, phase, k, q], recv.at[s, phase, k, q],
                       torus.device(torus.moved(pos, BACK[s // 2][phase], d), core))
 
     def last(s, by):
@@ -419,51 +437,110 @@
 
         lax.fori_loop(0, nzl * nzh * ny, one, 0)
 
-    def cross(t):
-        o, hh = t // 2, t % 2
+    def cross(o, hh):
+        t = 2 * o + hh
         zs, os = pl.ds(hh * hz, hz), pl.ds(2 * o, 2)
         return remote(part.at[1 - core, :, zs, :, os], theirs.at[:, zs, :, os], sib_send.at[t], sib_recv.at[t], sibling)
 
     everywhere = {"x": None, "y": None, "z": None}
 
     def begin(o):
-        for t in (2 * o, 2 * o + 1):
-            cross(t).wait_recv()
+        for hh in range(2):
+            cross(o, hh).wait_recv()
         for s in (2 * o, 2 * o + 1):
             add(s, everywhere, theirs.at[:, :, :, s], None)
-            for h in range(2):
-                ring(s, 0, 0, h).start()
+            for q in range(n[BACK[s // 2][1]]):
+                ring(s, 0, 0, q).start()
+
+    begun, past, sent = [], set(), set()
+
+    def events():
+        out = []
+        for s in range(NS):
+            o = s // 2
+            a, b, c = (n[x] for x in BACK[o])
+            size = volume(torus, BACK[o][2:]) * 0.35
+            at = (19.0, 31.0, 42.0)[o]
+            when = [at] * b
+            for k in range(a - 1):
+                for q in range(b):
+                    at = max(at, when[q] + 2.0) + size
+                    when[q] = at
+                    out.append((at, s, 0, k, q))
+            at = 0.0
+            for k in range(b - 1):
+                at = max(at, when[k]) + size + 2.0
+                out.append((at, s, 1, k, 0))
+            out.append((max(at, when[b - 1]) + 6.0, s, 2, 0, 0))
+        return sorted(out)
+
+    def handle(event):
+        _, s, phase, k, q = event
+        order = BACK[s // 2]
+        a, b, c = (n[x] for x in order)
+        d = 1 if s % 2 == 0 else -1
+        if phase < 2:
+            ring(s, phase, k, q).wait_recv()
+            add(s, spot(s, phase, -d * (k + 2), q), slot(s, phase, k, q), None)
+            if phase == 0 and k + 1 < a - 1:
+                ring(s, 0, k + 1, q).start()
+        else:
+            zl, zh = torus.split(pos["z"])
+            col = pl.ds(pl.multiple_of(pos["x"] * width, LANE), width)
+            total = part[core, zl, zh, pos["y"], s, :, col].astype(F32)
+            for by in range(1, c):
+                last(s, by).wait_recv()
+                total = total + bufs[s // 2 * 3 + 2][s % 2, by - 1].astype(F32)
+            fin[s * OCT:(s + 1) * OCT, :] = total
+        past.add((s, phase, k, q))
+        for j in range(b):
+            ready = (s, 0, a - 2, j) in past and (j == 0 or (s, 1, j - 1, 0) in past)
+            if ready and (s, j) not in sent:
+                sent.add((s, j))
+                if j < b - 1:
+                    ring(s, 1, j, 0).start()
+                else:
+                    for by in range(1, c):
+                        last(s, by).start()
+
+    todo = events()
 
     def rows_phase(xs, ds, x_sem, d_sem):
-        def fetch(which, t):
-            o, hh = t // 2, t % 2
+        def fetch(which, o, hh):
             buf, sem = (xs, x_sem) if which == 0 else (ds, d_sem)
             return [pltpu.make_async_copy(every.at[which, d, pl.ds(hh * hz, hz), :, :, o], buf.at[d], sem.at[d])
                     for d in range(2)]
 
         for which in range(2):
-            for c in fetch(which, 0):
+            for c in fetch(which, 0, 0):
                 c.start()
         score[...] = jnp.zeros_like(score)
         torus.greet(pos, core)
         for c in loads:
             c.wait()
-        for t in range(tiles):
-            o, hh = t // 2, t % 2
-            for c in fetch(0, t):
+        def tile(o, hh, carry):
+            t = 2 * o + hh
+
+            def ahead(which):
+                if o < NS // 2 - 1:
+                    for c in fetch(which, o + hh, 1 - hh):
+                        c.start()
+                else:
+                    @pl.when(hh == 0)
+                    def _():
+                        for c in fetch(which, o, 1):
+                            c.start()
+
+            for c in fetch(0, o, hh):
                 c.wait()
             pre = jnp.dot(xs[0].reshape(rows, half), wcat[:half, :], preferred_element_type=F32)
             pre = pre + jnp.dot(xs[1].reshape(rows, half), wcat[half:, :], preferred_element_type=F32)
-            if t + 1 < tiles:
-                for c in fetch(0, t + 1):
-                    c.start()
-            for c in fetch(1, t):
+            ahead(0)
+            for c in fetch(1, o, hh):
                 c.wait()
             back = lax.dot_general(ds[0].reshape(rows, half), wdown[:, :half], NT, preferred_element_type=F32)
             back = back + lax.dot_general(ds[1].reshape(rows, half), wdown[:, half:], NT, preferred_element_type=F32)
-            if t + 1 < tiles:
-                for c in fetch(1, t + 1):
-                    c.start()
+            ahead(1)
             gate_pre, up_pre = pre[:, :LANE], pre[:, LANE:]
             scale = gates[t]
             sigma = jax.nn.sigmoid(gate_pre)
@@ -472,7 +549,7 @@
             dact = scale * back
             grad_gate = dact * up_pre * sigma * (1.0 + gate_pre * (1.0 - sigma))
             grad_up = dact * silu
-            cols = pl.ds(t * rows, rows)
+            cols = pl.ds(pl.multiple_of(t * rows, rows), rows)
             gt[:LANE, cols] = grad_gate.T.astype(BF16)
             gt[LANE:, cols] = grad_up.T.astype(BF16)
             wt[:, cols] = (scale * act).T.astype(BF16)
@@ -485,10 +562,20 @@
                 grad = lax.dot_general(both, wcat[j * width:(j + 1) * width, :], NT, preferred_element_type=F32)
                 grad = grad.reshape(hz, n["y"], 2, 2, OCT, width).astype(BF16)
                 for k in range(2):
-                    part[k, zl, hh * hz:(hh + 1) * hz, :, 2 * o:2 * o + 2, :, x * width:(x + 1) * width] = grad[:, :, k]
-            cross(t).start()
-            if t in (2, 4):
-                begin(t // 2 - 1)
+                    part[k, zl, pl.ds(hh * hz, hz), :, 2 * o:2 * o + 2, :, x * width:(x + 1) * width] = grad[:, :, k]
+            cross(o, hh).start()
+            if o > 0:
+                @pl.when(hh == 0)
+                def _():
+                    begin(o - 1)
+            return carry
+
+        for o in range(NS // 2):
+            lax.fori_loop(0, 2, functools.partial(tile, o), 0)
+            if o > 0:
+                begun.extend((2 * o - 2, 2 * o - 1))
+            while todo and todo[0][1] in begun and todo[0][0] < 12.0 * (o + 1) + 1.0:
+                handle(todo.pop(0))
 
     pl.run_scoped(
         rows_phase,
@@ -555,51 +642,19 @@
 
         get(0)
         begin(2)
-        events = []
-        for s in range(NS):
-            order = BACK[s // 2]
-            at = (s // 2) * 3.0
-            for phase in (0, 1):
-                w = volume(torus, order[phase + 1:])
-                for k in range(n[order[phase]] - 1):
-                    for h in range(2):
-                        at += w / 2 + 0.5
-                        events.append((at, s, phase, k, h))
-                at += 2.0
-            events.append((at + 6.0, s, 2, 0, 0))
-        events.sort()
+        total = len(todo)
         done = 0
-        for i, (_, s, phase, k, h) in enumerate(events):
+        for i, event in enumerate(todo):
             if i == 4:
                 for q, offset in enumerate(torus.experts()):
                     message(q, offset, -1).wait_recv()
                 for q, offset in enumerate(torus.peers()):
                     share(q, offset, 1).start()
                 score_all[my_et] = score_in[...]
-            while done < units and done * len(events) * 3 // 5 <= i * units:
+            while done < units - 2 and done * total * 3 // 5 <= i * (units - 2):
                 unit(done)
                 done += 1
-            order = BACK[s // 2]
-            d = 1 if s % 2 == 0 else -1
-            if phase < 2:
-                ring(s, phase, k, h).wait_recv()
-                add(s, place(s, phase, -d * (k + 2)), slot(s, phase, k, h), h)
-                if k + 1 < n[order[phase]] - 1:
-                    ring(s, phase, k + 1, h).start()
-                elif h == 1 and phase == 0:
-                    for hh in range(2):
-                        ring(s, 1, 0, hh).start()
-                elif h == 1:
-                    for by in range(1, n[order[2]]):
-                        last(s, by).start()
-            else:
-                zl, zh = torus.split(pos["z"])
-                col = pl.ds(pl.multiple_of(pos["x"] * width, LANE), width)
-                total = part[core, zl, zh, pos["y"], s, :, col].astype(F32)
-                for by in range(1, n[order[2]]):
-                    last(s, by).wait_recv()
-                    total = total + bufs[s // 2 * 3 + 2][s % 2, by - 1].astype(F32)
-                fin[s * OCT:(s + 1) * OCT, :] = total
+            handle(event)
         count = out.shape[1]
         for i in range(out.shape[0]):
             ship[i] = fin[i * count:(i + 1) * count, :].astype(BF16)
@@ -630,13 +685,13 @@
     for q, offset in enumerate(torus.experts()):
         message(q, offset, 1).wait_send()
     for t in range(tiles):
-        cross(t).wait_send()
+        cross(t // 2, t % 2).wait_send()
     for s in range(NS):
         order = BACK[s // 2]
         for phase in (0, 1):
             for k in range(n[order[phase]] - 1):
-                for h in range(2):
-                    ring(s, phase, k, h).wait_send()
+                for q in range(n[order[1]] if phase == 0 else 1):
+                    ring(s, phase, k, q).wait_send()
         for by in range(1, n[order[2]]):
             last(s, by).wait_send()
 
@@ -650,8 +705,10 @@
     bufs = []
     for order in BACK:
         for phase, axis in enumerate(order):
-            free = order[phase + 1:]
+            free = order[2:] if phase < 2 else ()
             shape = (2, n[axis] - 1)
+            if phase == 0:
+                shape += (n[order[1]],)
             if "z" in free:
                 shape += (torus.nzl, torus.nzh)
             if "y" in free:
@@ -681,7 +738,7 @@
                         vm((2 * LANE, total), BF16), vm((LANE, total), BF16), vm((experts, 1, LANE), F32),
                         vm((experts, 1, LANE), F32), vm((n_et, experts, 1, LANE), F32), vm((NS * OCT, width), F32),
                         vm(owned, BF16), vm(owned, BF16), *bufs, dma((3,)), dma((NS,)), dma((NS,)),
-                        dma((NS, 2, most, 2)), dma((NS, 2, most, 2)), dma((NS, most)), dma((NS, most)),
+                        dma((NS, 2, most, 4)), dma((NS, 2, most, 4)), dma((NS, most)), dma((NS, most)),
                         dma((others,)), dma((others,)), dma((peers,)), dma((peers,)), dma((peers,)), dma((peers,))],
         compiler_params=pltpu.CompilerParams(
             collective_id=1, has_side_effects=True, vmem_limit_bytes=67043328),

time: 253 us -> 275 us (1.087)
  Pallas kernels: 235 us -> 257 us
    pallas_call x1, Pallas kernels: 114 us -> 128 us  [back_all(): pl.pallas_call(functools.partial(back_kernel, torus, depth, min(512, dept...]
    pallas_call x1, Pallas kernels: 121 us -> 129 us  [gather_all(): pl.pallas_call(functools.partial(gather_kernel, torus, width), out_shape=...]
where the time goes in v4:
time: 275 us
  Pallas kernels  257 us (93%)
  local copies, waits for them, and re-layouts  14.6 us (5%)
    pallas_call x1, Pallas kernels, gather_all(): pl.pallas_call(functools.partial(gather_kernel, torus, width), out_shape=...  129 us
    pallas_call x1, Pallas kernels, back_all(): pl.pallas_call(functools.partial(back_kernel, torus, depth, min(512, dept...  128 us
    unnamed x12, local copies, waits for them, and re-layouts  7.93 us

profile of v4, /device:TPU:32, one launch (start us, length us, event | category | flops | bytes accessed | tf_op | source)
XLA Modules:
  0.0 275.0 jit_solution(394425383118919404)
XLA Ops:
  0.7 1.0 stack.9
  1.7 1.0 stack.10
  2.8 0.2 maximum_bitcast_fusion
  3.0 0.1 reshape.32
  3.1 0.7 copy.28.packed
  3.8 0.1 select_reduce_fusion.1
  3.9 0.1 copy.27
  4.1 0.6 pad_convert_fusion
  4.7 129.1 %gather_all.1 = (bf16[2,2,4,4,2,3,16,3584]{7,6,5,4,3,2,1,0:T(8,128)(2,1)}, f32[8,32,1,128]{3,2,1,0:T(1,128)}) custom-call(bf16[8,6,1792]{2,1,0:T(8,128)(2,1)} %copy.28.packed, f32[32,1,128]{2,1,0:T(1,128)} %bitcast.36), custom_call_target="tpu_custom_call" | custom-call | tf_op jit(solution)/shard_map/gather_all/pallas_call | solution.py:317
  133.8 1.0 copy.29
  134.8 0.1 reshape.33
  134.9 0.1 copy.30
  135.0 0.1 broadcast_in_dim.53
  135.1 1.1 broadcast_in_dim.54.gates
  136.2 128.2 %back_all.1 = (bf16[8,6,896]{2,1,0:T(8,128)(2,1)}, f32[8,32,1,128]{3,2,1,0:T(1,128)}, bf16[7168,128]{1,0:T(8,128)(2,1)}, bf16[7168,128]{1,0:T(8,128)(2,1)}, bf16[128,7168]{1,0:T(8,128)(2,1)}) custom-call(bf16[2,2,4,4,2,3,16,3584]{7,6,5,4,3,2,1,0:T(8,128)(2,1)} %get-tuple-element.12.every, f32[6,256,128]{2,1,0:T(8,128)} %broadcast_in_dim.54.gates, ...), custom_call_target="tpu_custom_call" | custom-call | tf_op jit(solution)/shard_map/back_all/pallas_call | solution.py:728
  264.4 1.0 slice.16
  265.4 0.1 copy.31
  265.6 0.8 iota_compare_fusion
  266.4 0.7 select_reduce_fusion
  267.1 1.6 copy.36
  268.6 3.0 %copy.37 = bf16[1,7168,128]{2,1,0:T(8,128)(2,1)} copy(bf16[1,7168,128]{2,1,0:T(8,128)(2,1)} %bitcast.28) | data formatting | bytes 3670016
  271.6 1.2 copy.38
  272.8 0.9 copy-done
  273.8 1.2 copy.39
  (12 shorter events, 0.2 us)
Async XLA Ops:
  0.6 3.2 %copy-start.3 = (bf16[6,8]{1,0:T(8,128)(2,1)S(1)}, bf16[6,8]{1,0:T(8,128)(2,1)}, u32[]{:S(2)}) copy-start(bf16[6,8]{1,0:T(8,128)(2,1)} %param.9) | copy-start | bytes 292
  0.6 3.2 %copy-start.2 = (s32[6,8]{1,0:T(8,128)S(1)}, s32[6,8]{1,0:T(8,128)}, u32[]{:S(2)}) copy-start(s32[6,8]{1,0:T(8,128)} %param.10) | copy-start | bytes 580
  268.6 3.0 %copy-start.1 = (bf16[7168,128]{1,0:T(8,128)(2,1)S(1)}, bf16[7168,128]{1,0:T(8,128)(2,1)}, u32[]{:S(2)}) copy-start(bf16[7168,128]{1,0:T(8,128)(2,1)} %get-tuple-element.17) | copy-start | bytes 5505028
  271.6 2.2 copy-start

commit v5 on v3

--- a/solution.py
+++ b/solution.py
@@ -240,14 +240,14 @@
     events = []
     for s in range(NS):
         order = ORDERS[s // 2]
-        at = 0.0
+        at = 20.0 if order[0] == "x" else 30.0
         for phase in (1, 2):
-            w = volume(torus, order[:phase]) * (1.5 if phase == 1 else 1.0)
+            w = volume(torus, order[:phase]) * 0.66
             for k in range(torus.n[order[phase]] - 1):
                 for part in range(2):
-                    at += w / 2 + 0.5
+                    at += w / 2 + (0.8 if phase == 1 else 0.3)
                     events.append((at, s, phase, k, part))
-            at += 1.0
+            at += 1.5
     for _, s, phase, k, part in sorted(events):
         order = ORDERS[s // 2]
         arrived = landed(s, phase, k, part)
@@ -554,11 +554,10 @@
                 c.start()
 
         get(0)
-        begin(2)
         events = []
         for s in range(NS):
             order = BACK[s // 2]
-            at = (s // 2) * 3.0
+            at = (0.0, 5.0, 12.0)[s // 2]
             for phase in (0, 1):
                 w = volume(torus, order[phase + 1:])
                 for k in range(n[order[phase]] - 1):
@@ -571,12 +570,13 @@
         done = 0
         for i, (_, s, phase, k, h) in enumerate(events):
             if i == 4:
+                begin(2)
                 for q, offset in enumerate(torus.experts()):
                     message(q, offset, -1).wait_recv()
                 for q, offset in enumerate(torus.peers()):
                     share(q, offset, 1).start()
                 score_all[my_et] = score_in[...]
-            while done < units and done * len(events) * 3 // 5 <= i * units:
+            while i >= 4 and done < units - 2 and done * len(events) * 3 // 5 <= i * (units - 2):
                 unit(done)
                 done += 1
             order = BACK[s // 2]

time: 253 us -> 253 us (level)
    pallas_call x1, Pallas kernels: 121 us -> 124 us  [gather_all(): pl.pallas_call(functools.partial(gather_kernel, torus, width), out_shape=...]
    pallas_call x1, Pallas kernels: 114 us -> 111 us  [back_all(): pl.pallas_call(functools.partial(back_kernel, torus, depth, min(512, dept...]
where the time goes in v5:
time: 253 us
  Pallas kernels  235 us (93%)
  local copies, waits for them, and re-layouts  14.6 us (6%)
    pallas_call x1, Pallas kernels, gather_all(): pl.pallas_call(functools.partial(gather_kernel, torus, width), out_shape=...  124 us
    pallas_call x1, Pallas kernels, back_all(): pl.pallas_call(functools.partial(back_kernel, torus, depth, min(512, dept...  111 us
    unnamed x12, local copies, waits for them, and re-layouts  7.93 us

profile of v5, /device:TPU:32, one launch (start us, length us, event | category | flops | bytes accessed | tf_op | source)
XLA Modules:
  0.0 252.8 jit_solution(16120607665008543368)
XLA Ops:
  0.7 1.0 stack.9
  1.7 1.0 stack.10
  2.8 0.2 maximum_bitcast_fusion
  3.0 0.1 reshape.32
  3.1 0.7 copy.28.packed
  3.8 0.1 select_reduce_fusion.1
  3.9 0.1 copy.27
  4.1 0.6 pad_convert_fusion
  4.7 124.0 %gather_all.1 = (bf16[2,2,4,4,2,3,16,3584]{7,6,5,4,3,2,1,0:T(8,128)(2,1)}, f32[8,32,1,128]{3,2,1,0:T(1,128)}) custom-call(bf16[8,6,1792]{2,1,0:T(8,128)(2,1)} %copy.28.packed, f32[32,1,128]{2,1,0:T(1,128)} %bitcast.36), custom_call_target="tpu_custom_call" | custom-call | tf_op jit(solution)/shard_map/gather_all/pallas_call | solution.py:295
  128.7 1.0 copy.29
  129.8 0.1 reshape.33
  129.9 0.1 copy.30
  129.9 0.1 broadcast_in_dim.53
  130.0 1.1 broadcast_in_dim.54.gates
  131.2 111.1 %back_all.1 = (bf16[8,6,896]{2,1,0:T(8,128)(2,1)}, f32[8,32,1,128]{3,2,1,0:T(1,128)}, bf16[7168,128]{1,0:T(8,128)(2,1)}, bf16[7168,128]{1,0:T(8,128)(2,1)}, bf16[128,7168]{1,0:T(8,128)(2,1)}) custom-call(bf16[2,2,4,4,2,3,16,3584]{7,6,5,4,3,2,1,0:T(8,128)(2,1)} %get-tuple-element.12.every, f32[6,256,128]{2,1,0:T(8,128)} %broadcast_in_dim.54.gates, ...), custom_call_target="tpu_custom_call" | custom-call | tf_op jit(solution)/shard_map/back_all/pallas_call | solution.py:671
  242.3 1.0 slice.16
  243.3 0.1 copy.31
  243.5 0.8 iota_compare_fusion
  244.2 0.7 select_reduce_fusion
  244.9 1.6 copy.36
  246.5 3.0 %copy.37 = bf16[1,7168,128]{2,1,0:T(8,128)(2,1)} copy(bf16[1,7168,128]{2,1,0:T(8,128)(2,1)} %bitcast.28) | data formatting | bytes 3670016
  249.4 1.2 copy.38
  250.7 0.9 copy-done
  251.6 1.2 copy.39
  (12 shorter events, 0.2 us)
Async XLA Ops:
  0.6 3.2 %copy-start.3 = (bf16[6,8]{1,0:T(8,128)(2,1)S(1)}, bf16[6,8]{1,0:T(8,128)(2,1)}, u32[]{:S(2)}) copy-start(bf16[6,8]{1,0:T(8,128)(2,1)} %param.9) | copy-start | bytes 292
  0.6 3.2 %copy-start.2 = (s32[6,8]{1,0:T(8,128)S(1)}, s32[6,8]{1,0:T(8,128)}, u32[]{:S(2)}) copy-start(s32[6,8]{1,0:T(8,128)} %param.10) | copy-start | bytes 580
  246.5 3.0 %copy-start.1 = (bf16[7168,128]{1,0:T(8,128)(2,1)S(1)}, bf16[7168,128]{1,0:T(8,128)(2,1)}, u32[]{:S(2)}) copy-start(bf16[7168,128]{1,0:T(8,128)(2,1)} %get-tuple-element.17) | copy-start | bytes 5505028
  249.4 2.2 copy-start
